TPU v7x, 32 devices: a whole 2x2x4 slice. The times are simulated.
32 devices in a mesh: dp: 2 (over x), ctx: 16 (over z, y, core).
Axes of the slice: x: 2, y: 2, z: 4, core: 2. Of those that a mesh axis runs over, the one named last changes fastest.
Arguments:
- inputs: bfloat16 [2, 2048, 1024], P('dp', 'ctx'), may hold values from -6 to 6
- cotangent: bfloat16 [2, 2048, 1024], P('dp', 'ctx'), may hold values from -6 to 6
- block_ids: int32 [2, 2048], P('dp', 'ctx'), may hold values from 0 to 15, never falling along the last dimension, each value on 1 to 256 neighbouring positions
- ln1_gain: bfloat16 [1024], P(('dp', 'ctx')), may hold values from 0.5 to 1.5
- ln1_bias: bfloat16 [1024], P(('dp', 'ctx')), may hold values from -3 to 3
- w_qkv: bfloat16 [1024, 3072], P(('dp', 'ctx')), may hold values from -0.1875 to 0.1875
- b_qkv: bfloat16 [2048], P(('dp', 'ctx')), may hold values from -3 to 3
- w_out: bfloat16 [1024, 1024], P(('dp', 'ctx')), may hold values from -1.5 to 1.5
- b_out: bfloat16 [1024], P(('dp', 'ctx')), may hold values from -3 to 3
- ln2_gain: bfloat16 [1024], P(('dp', 'ctx')), may hold values from 0.5 to 1.5
- ln2_bias: bfloat16 [1024], P(('dp', 'ctx')), may hold values from -3 to 3
- w_fc: bfloat16 [1024, 4096], P(('dp', 'ctx')), may hold values from -0.1875 to 0.1875
- b_fc: bfloat16 [4096], P(('dp', 'ctx')), may hold values from -3 to 3
- w_proj: bfloat16 [4096, 1024], P(('dp', 'ctx')), may hold values from -0.09375 to 0.09375
- b_proj: bfloat16 [1024], P(('dp', 'ctx')), may hold values from -3 to 3
Outputs:
- output: bfloat16 [2, 2048, 1024], P('dp', 'ctx')
- input_grad: bfloat16 [2, 2048, 1024], P('dp', 'ctx')
- ln1_gain_grad: float32 [1024], P(('dp', 'ctx'))
- ln1_bias_grad: float32 [1024], P(('dp', 'ctx'))
- w_qkv_grad: float32 [1024, 3072], P(('dp', 'ctx'))
- b_qkv_grad: float32 [2048], P(('dp', 'ctx'))
- w_out_grad: float32 [1024, 1024], P(('dp', 'ctx'))
- b_out_grad: float32 [1024], P(('dp', 'ctx'))
- ln2_gain_grad: float32 [1024], P(('dp', 'ctx'))
- ln2_bias_grad: float32 [1024], P(('dp', 'ctx'))
- w_fc_grad: float32 [1024, 4096], P(('dp', 'ctx'))
- b_fc_grad: float32 [4096], P(('dp', 'ctx'))
- w_proj_grad: float32 [4096, 1024], P(('dp', 'ctx'))
- b_proj_grad: float32 [1024], P(('dp', 'ctx'))
Inputs may be any that keep to these rules, and one draw needn't show every extreme that they name: `block_ids`: in each sequence the block numbers start at 0, never fall from one token to the next and rise in steps of one; each block has 1 to 256 tokens, and some block has exactly 256.
All inputs are finite; a program needn't handle non-finite values.
Results may differ from a plain program's by a relative error of at most 0.017.
Values may be sent and summed in bfloat16 or wider, within the bound.
A program may use at most 192 MiB of HBM per device.

v0:
```python
import functools
import math

import jax
import jax.numpy as jnp
from jax import lax
from jax.experimental import pallas as pl
from jax.experimental.pallas import tpu as pltpu
from jax.sharding import PartitionSpec as P

HEADS = 16
EPSILON = 1e-05
QB = 256
F32, BF16 = jnp.float32, jnp.bfloat16
NT = (((1,), (1,)), ((), ()))
TN = (((0,), (0,)), ((), ()))
MESH = pl.DeviceIdType.MESH
DMA = pltpu.SemaphoreType.DMA
VMEM_LIMIT = 60 << 20


def dot(x, y, dims=(((1,), (0,)), ((), ()))):
    return lax.dot_general(x, y, dims, preferred_element_type=F32)


def remote(src, dst, send, recv, peer):
    return pltpu.make_async_remote_copy(
        src_ref=src, dst_ref=dst, send_sem=send, recv_sem=recv, device_id=peer, device_id_type=MESH
    )


class Greet:
    def __init__(self, n_dp, n, peers=None):
        self.barrier = pltpu.get_barrier_semaphore()
        self.count = n_dp * n - 1 if peers is None else len(peers)
        for peer in peers or ():
            pl.semaphore_signal(self.barrier, inc=1, device_id=peer, device_id_type=MESH)
        if peers is None:
            flat = lax.axis_index("dp") * n + lax.axis_index("ctx")

            def signal(j, _):
                f = lax.rem(flat + j, n_dp * n)
                pl.semaphore_signal(self.barrier, inc=1, device_id={"dp": f // n, "ctx": f % n}, device_id_type=MESH)
                return 0

            lax.fori_loop(1, n_dp * n, signal, 0)

    def wait(self):
        pl.semaphore_wait(self.barrier, self.count)


class ToAll:
    def __init__(self, n_dp, n, block, into, sems, only_ctx=False):
        self.n, self.block, self.into, self.only = n, block, into, only_ctx
        self.send, self.recv = sems
        self.count = n if only_ctx else n_dp * n
        self.me = lax.axis_index("ctx") if only_ctx else lax.axis_index("dp") * n + lax.axis_index("ctx")

    def copy(self, j):
        f = lax.rem(self.me + j, self.count)
        peer = {"ctx": f} if self.only else {"dp": f // self.n, "ctx": f % self.n}
        return remote(self.block(f), self.into.at[self.me], self.send.at[j], self.recv.at[j], peer)

    def each(self, act):
        def step(j, _):
            act(self.copy(j))
            return 0

        lax.fori_loop(1, self.count, step, 0)

    def start(self):
        self.each(lambda c: c.start())

    def wait_recv(self):
        self.each(lambda c: c.wait_recv())

    def wait_send(self):
        self.each(lambda c: c.wait_send())


def own_bit(dim):
    axis, b = dim
    return lax.axis_index(axis) // (1 << b) % 2


def partner(dim):
    axis, b = dim
    return {axis: lax.axis_index(axis) + (1 - 2 * own_bit(dim)) * (1 << b)}


def cube_plan(n, rows):
    top = n.bit_length() - 2
    dims = [("dp", 0)] + [("ctx", b) for b in range(top - 1, 0, -1)] + [("ctx", 0)]
    links = len(dims) - 1
    size = -(-rows // (16 * links)) * 16
    cuts = [min(rows, size * i) for i in range(links)] + [rows]
    return dims, [(cuts[i], cuts[i + 1], [(i + j) % links for j in range(links)]) for i in range(links)], True


def all_plan(n_dp, n, rows):
    dims = [("dp", b) for b in range(n_dp.bit_length() - 2, -1, -1)] + [("ctx", b) for b in range(n.bit_length() - 2, -1, -1)]
    links, own = len(dims) - 1, n_dp.bit_length() - 1
    return dims, [(0, rows, list(range(own, links)) + list(range(own)))], False


class Pairwise:
    def __init__(self, plan, sems):
        self.dims, self.orders, self.core_first = plan
        self.links = len(self.dims) - 1
        self.link_send, self.link_recv, self.core_send, self.core_recv = sems
        self.mine = [own_bit(d) for d in self.dims]

    def index(self, links, core, tail=()):
        links = tuple(links)
        return ((core,) + links if self.core_first else links + (core,)) + tuple(tail)

    def peers(self):
        return [partner(d) for d in self.dims]


class Gather(Pairwise):
    def __init__(self, plan, buf, sems):
        super().__init__(plan, sems)
        self.buf = buf

    @staticmethod
    def sems(plan):
        links, parts = len(plan[0]) - 1, len(plan[1])
        return [DMA((parts, links))] * 2 + [DMA((parts * links + 1,))] * 2

    def own(self):
        return self.index(self.mine[:-1], self.mine[-1])

    def region(self, part, done, flip=None):
        lo, hi, _ = self.orders[part]
        where = [slice(None) if i in done else (1 - m if i == flip else m) for i, m in enumerate(self.mine[:-1])]
        return self.index(where, self.mine[-1], (pl.ds(lo, hi - lo),))

    def copy(self, where, send, recv, dim):
        return remote(self.buf.at[where], self.buf.at[where], send, recv, partner(self.dims[dim]))

    def link(self, part, k):
        order = self.orders[part][2]
        return self.copy(self.region(part, order[:k]), self.link_send.at[part, k], self.link_recv.at[part, k], order[k])

    def core(self, part, k):
        order = self.orders[part][2]
        at = part * self.links + k + 1
        return self.copy(self.region(part, order[:k], order[k]), self.core_send.at[at], self.core_recv.at[at], self.links)

    def core_own(self):
        return self.copy(self.own(), self.core_send.at[0], self.core_recv.at[0], self.links)

    def start(self):
        for part in range(len(self.orders)):
            self.link(part, 0).start()
        self.core_own().start()

    def step(self, k):
        for part in range(len(self.orders)):
            self.link(part, k).wait_recv()
            if k + 1 < self.links:
                self.link(part, k + 1).start()
            self.core(part, k).start()

    def core_wait(self):
        self.core_own().wait_recv()
        for part in range(len(self.orders)):
            for k in range(self.links):
                self.core(part, k).wait_recv()

    def finish(self):
        self.core_own().wait_send()
        for part in range(len(self.orders)):
            for k in range(self.links):
                self.link(part, k).wait_send()
                self.core(part, k).wait_send()


class Scatter(Pairwise):
    def __init__(self, plan, terms, bufs, sems, own=None):
        super().__init__(plan, sems)
        self.terms, self.run, self.bufs, self.own = terms, bufs[0], bufs[1:], own

    def fetch_own(self, sem):
        source = self.terms.at[self.index((slice(None),) * self.links, self.mine[-1])]
        return pltpu.make_async_copy(source, self.own, sem)

    @staticmethod
    def sems(plan):
        links, parts = len(plan[0]) - 1, len(plan[1])
        return [DMA((parts, links))] * 2 + [DMA((2,))] * 2

    @staticmethod
    def scratch(plan, rows, cols):
        links = len(plan[0]) - 1
        return [pltpu.VMEM((2,) * links + (rows, cols), BF16)] + [
            pltpu.VMEM((2,) * (links - 1 - k) + (rows, cols), BF16) for k in range(links)
        ]

    def core(self, half):
        where = (half,) + (slice(None),) * (self.links - 1)
        return remote(
            self.terms.at[self.index(where, 1 - self.mine[-1])], self.run.at[where],
            self.core_send.at[half], self.core_recv.at[half], partner(self.dims[-1]),
        )

    def where(self, part, k, flip):
        lo, hi, order = self.orders[part]
        order = order[::-1]
        d, gone = order[k], order[:k]
        at = []
        for i in range(self.links):
            if i == d:
                at.append(1 - self.mine[i] if flip else self.mine[i])
            else:
                at.append(self.mine[i] if i in gone else slice(None))
        return at, d, (pl.ds(lo, hi - lo),)

    def link(self, part, k):
        at, d, tail = self.where(part, k, True)
        return remote(
            self.run.at[tuple(at) + tail], self.bufs[k].at[(slice(None),) * (self.links - 1 - k) + tail],
            self.link_send.at[part, k], self.link_recv.at[part, k], partner(self.dims[d]),
        )

    def add_core(self, half):
        self.core(half).wait_recv()
        inner = self.links - 1
        for i in range(1 << inner):
            at = (half,) + tuple((i >> (inner - 1 - j)) & 1 for j in range(inner))
            own = self.terms[self.index(at, self.mine[-1])] if self.own is None else self.own[at]
            self.run[at] = (self.run[at].astype(F32) + own.astype(F32)).astype(BF16)

    def start_links(self):
        for part in range(len(self.orders)):
            self.link(part, 0).start()

    def step(self, k, out=None):
        for part in range(len(self.orders)):
            at, _, tail = self.where(part, k, False)
            self.link(part, k).wait_recv()
            free = self.links - 1 - k
            for i in range(1 << free):
                idx = [(i >> (free - 1 - j)) & 1 for j in range(free)]
                rest = iter(idx)
                to = tuple(next(rest) if isinstance(v, slice) else v for v in at) + tail
                total = self.run[to].astype(F32) + self.bufs[k][tuple(idx) + tail].astype(F32)
                if k + 1 < self.links:
                    self.run[to] = total.astype(BF16)
                else:
                    out[tail[0], :] = total
            if k + 1 < self.links:
                self.link(part, k + 1).start()

    def finish(self):
        for half in range(2):
            self.core(half).wait_send()
        for part in range(len(self.orders)):
            for k in range(self.links):
                self.link(part, k).wait_send()


class Line:
    def __init__(self, n):
        self.n, self.ys = n, n // 8
        me = lax.axis_index("ctx")
        self.z, self.y, self.c = me // (2 * self.ys), me // 2 % self.ys, me % 2
        high = self.z // 2
        self.slots = [3 - 3 * high, 2 - high, self.z + 1 - 2 * (self.z % 2), self.z]
        self.inner = (self.z == 1) | (self.z == 2)
        self.outer = (self.z == 0) | (self.z == 3)
        self.side = (self.z + 1) // 2 % 2
        self.near = self.at(self.slots[2], self.y, self.c)
        self.far = self.at(self.z + 1 - 2 * high, self.y, self.c)
        self.core = self.at(self.z, self.y, 1 - self.c)

    def at(self, z, y, c):
        return {"ctx": (z * self.ys + y) * 2 + c}

    def others(self):
        return [(self.y + d) % self.ys for d in range(1, self.ys)]


class LineGather:
    def __init__(self, line, buf, sems):
        self.l, self.buf = line, buf
        self.zs, self.zr, self.ys, self.yr, self.ks, self.kr = sems

    @staticmethod
    def sems(n):
        ys = n // 8
        return [DMA((5,)), DMA((3,)), DMA((ys - 1, 4)), DMA((ys - 1, 4)), DMA((ys, 4)), DMA((ys, 4))]

    def move(self, z, y, c, send, recv, peer):
        ref = self.buf.at[z, y, c]
        return remote(ref, ref, send, recv, peer)

    def zcopy(self, i):
        l = self.l
        slot, peer, into = [(3, l.near, 0), (3, l.far, 1), (2, l.far, 2), (1, l.near, 1), (0, l.near, 2)][i]
        return self.move(l.slots[slot], l.y, l.c, self.zs.at[i], self.zr.at[into], peer)

    def ycopy(self, d, slot):
        l = self.l
        return self.move(l.slots[slot], l.y, l.c, self.ys.at[d, slot], self.yr.at[d, slot], l.at(l.z, l.others()[d], l.c))

    def kcopy(self, d, slot):
        l = self.l
        y = l.y if d == 0 else (l.y + l.ys - d) % l.ys
        return self.move(l.slots[slot], y, l.c, self.ks.at[d, slot], self.kr.at[d, slot], l.core)

    def spread(self, slot):
        for d in range(self.l.ys - 1):
            self.ycopy(d, slot).start()
        self.kcopy(0, slot).start()

    def start(self):
        self.zcopy(0).start()

        @pl.when(self.l.inner)
        def _():
            self.zcopy(1).start()

        self.spread(3)

    def z_step(self, r):
        self.zcopy((0, 3, 4)[r]).wait_recv()

        @pl.when(self.l.inner)
        def _():
            self.zcopy(2 + r).start()

        self.spread(2 - r)

    def y_step(self, slot):
        for d in range(self.l.ys - 1):
            self.ycopy(d, slot).wait_recv()
            self.kcopy(d + 1, slot).start()

    def run(self):
        self.start()
        for r in range(3):
            self.z_step(r)
            self.y_step(3 - r)
        self.y_step(0)

    def core_wait(self, slot):
        for d in range(self.l.ys):
            self.kcopy(d, slot).wait_recv()

    def finish(self):
        self.zcopy(0).wait_send()

        @pl.when(self.l.inner)
        def _():
            for i in range(1, 5):
                self.zcopy(i).wait_send()

        for slot in range(4):
            for d in range(self.l.ys - 1):
                self.ycopy(d, slot).wait_send()
            for d in range(self.l.ys):
                self.kcopy(d, slot).wait_send()


class LineScatter:
    def __init__(self, line, acc, kbuf, ybuf, zbuf, sems):
        self.l, self.acc, self.kbuf, self.ybuf, self.zbuf = line, acc, kbuf, ybuf, zbuf
        self.zs, self.zr, self.ys, self.yr, self.ks, self.kr = sems

    @staticmethod
    def sems(n):
        ys = n // 8
        return [DMA((3,)), DMA((2, 3)), DMA((ys - 1, 4)), DMA((ys - 1, 4)), DMA((ys, 4)), DMA((ys, 4))]

    @staticmethod
    def scratch(n, rows, cols):
        ys = n // 8
        return [pltpu.VMEM((4, ys, rows, cols), BF16), pltpu.VMEM((ys - 1, 4, rows, cols), BF16), pltpu.VMEM((2, 3, rows, cols), BF16)]

    def y_of(self, d):
        return self.l.y if d == 0 else self.l.others()[d - 1]

    def kcopy(self, d, slot):
        l = self.l
        z, y = l.slots[slot], self.y_of(d)
        return remote(self.acc.at[z, y, 1 - l.c], self.kbuf.at[z, y], self.ks.at[d, slot], self.kr.at[d, slot], l.core)

    def ycopy(self, d, slot):
        l = self.l
        z, y = l.slots[slot], self.y_of(d + 1)
        return remote(self.acc.at[z, y, l.c], self.ybuf.at[d, slot], self.ys.at[d, slot], self.yr.at[d, slot], l.at(l.z, y, l.c))

    def zcopy(self, slot):
        l = self.l
        return remote(self.acc.at[l.slots[slot], l.y, l.c], self.zbuf.at[l.side, slot], self.zs.at[slot], self.zr.at[l.side, slot], l.far if slot < 2 else l.near)

    def zwait(self, side, slot):
        buf = self.zbuf.at[side, slot]
        remote(buf, buf, self.zs.at[slot], self.zr.at[side, slot], self.l.near).wait_recv()
        return self.zbuf[side, slot].astype(F32)

    def own(self, slot):
        return (self.l.slots[slot], self.l.y, self.l.c)

    def core_start(self, slot):
        for d in range(self.l.ys - 1, -1, -1):
            self.kcopy(d, slot).start()

    def core_step(self, slot):
        l = self.l
        for d in list(range(1, l.ys)) + [0]:
            z, y = l.slots[slot], self.y_of(d)
            self.kcopy(d, slot).wait_recv()
            self.acc[z, y, l.c] = (self.acc[z, y, l.c].astype(F32) + self.kbuf[z, y].astype(F32)).astype(BF16)
            if d > 0:
                self.ycopy(d - 1, slot).start()

    def y_sum(self, slot):
        total = self.acc[self.own(slot)].astype(F32)
        for d in range(self.l.ys - 1):
            self.ycopy(d, slot).wait_recv()
            total = total + self.ybuf[d, slot].astype(F32)
        return total

    def z_step(self, slot):
        l, own = self.l, self.own(slot)
        total = self.y_sum(slot)
        self.acc[own] = total.astype(BF16)
        @pl.when(l.inner)
        def _():
            self.acc[own] = (self.acc[own].astype(F32) + self.zwait(*((0, slot) if slot < 2 else (1, 0)))).astype(BF16)

        self.zcopy(slot).start()

    def last(self, out):
        l = self.l
        out[...] = self.y_sum(3)

        @pl.when(l.inner)
        def _():
            out[...] += self.zwait(0, 2) + self.zwait(1, 1)

        @pl.when(l.outer)
        def _():
            out[...] += self.zwait(1, 2)

    def finish(self):
        for slot in range(4):
            for d in range(self.l.ys):
                self.kcopy(d, slot).wait_send()
            for d in range(self.l.ys - 1):
                self.ycopy(d, slot).wait_send()
        for slot in range(3):
            self.zcopy(slot).wait_send()


G1, C1, BQV, IDS, BO, G2, C2, BF, BP = range(9)


def put_ids(n, small_all, first, row, col):
    tokens = small_all.shape[2]
    for j in range(n):
        ids = small_all[first + j].astype(F32)[IDS : IDS + 1, :]
        row[:, j * tokens : (j + 1) * tokens] = ids
        col[j * tokens : (j + 1) * tokens, :] = jnp.transpose(jnp.broadcast_to(ids, (tokens, tokens)))[:, :1]


def half_row(tile_row, odd, high):
    lane = lax.broadcasted_iota(jnp.int32, tile_row.shape, 1)
    turned = pltpu.roll(tile_row, 64, 1)
    moved = jnp.where((odd == 1) == high, tile_row, turned)
    return jnp.where((lane >= 64) == high, moved, 0.0)


def normalize(rows):
    centred = rows - jnp.mean(rows, axis=-1, keepdims=True)
    rstd = lax.rsqrt(jnp.mean(centred * centred, axis=-1, keepdims=True) + EPSILON)
    return centred * rstd, rstd


def group_of(n, f):
    d, j = f // n, f % n
    return d % 2 * (n // 2) + j % (n // 2), d // 2 * 2 + j // (n // 2)


def group_peer(n, i, count):
    d, j = lax.axis_index("dp"), lax.axis_index("ctx")
    g = lax.rem(d // 2 * 2 + j // (n // 2) + i, count)
    return g, {"dp": g // 2 * 2 + d % 2, "ctx": g % 2 * (n // 2) + j % (n // 2)}


def put_small(pieces, tile, small_ref):
    tile[...] = jnp.zeros_like(tile)
    for k, piece in enumerate(pieces):
        tile[k : k + 1, : piece.shape[1]] = piece[...].astype(F32)
    small_ref[...] = tile[...].astype(BF16)


def put_params(count, width, small_all, prm, bqv):
    for size, ref in ((width // count, prm), (2 * width // count, bqv)):
        per = 128 // size
        for k in range(count // per):
            tile = small_all[k * per].astype(F32)
            for i in range(1, per):
                tile = tile + pltpu.roll(small_all[k * per + i].astype(F32), i * size, 1)
            if ref is prm:
                prm[:, k * 128 : (k + 1) * 128] = tile
            else:
                bqv[k : k + 1, :] = tile[BQV : BQV + 1]


def front_kernel(n_dp, n, r, cube, *refs):
    refs = list(refs)
    take = lambda k: [refs.pop(0) for _ in range(k)]
    x_ref, pieces, dy_ref = refs.pop(0), take(9), refs.pop(0)
    (wq_all,) = take(1)
    small_all, first_out, a_ref, b_ref, o_ref, att, dy_all = take(7)
    xbuf, first, prm, bqv, bias, idrow, idcol, packed, acc, tot, own_sems, first_sems, tile, small_ref = take(14)
    line_sems, small_sems, dy_sems, att_sems = take(6), take(2), take(4), take(2)
    tokens, width = x_ref.shape
    count = n_dp * n
    d, me = lax.axis_index("dp"), lax.axis_index("ctx")
    flat = d * n + me
    head, part = me // r, me % r
    line = Line(n)
    hello = Greet(n_dp, n)

    xg = LineGather(line, xbuf, line_sems)
    small = ToAll(n_dp, n, lambda f: small_ref, small_all, small_sems)
    dyg = Gather(cube, dy_all, dy_sems)
    own_copies = [pltpu.make_async_copy(dy_ref, dy_all.at[dyg.own()], own_sems.at[0])]
    for c in own_copies:
        c.start()
    xbuf[line.z, line.y, line.c] = x_ref[...]
    put_small(pieces, tile, small_ref)
    small_all[flat] = small_ref[...]
    hello.wait()
    xg.start()
    small.start()
    for c in own_copies:
        c.wait()
    xg.z_step(0)
    xg.y_step(3)
    small.wait_recv()
    put_params(count, width, small_all, prm, bqv)
    odd = head % 2
    bias[:, :128] = half_row(bqv[pl.ds(head // 2, 1), :], odd, False)
    bias[:, 128:] = half_row(bqv[pl.ds(width // 128 + head // 2, 1), :], odd, True)
    put_ids(n, small_all, d * n, idrow, idcol)
    per_z = n // 4

    def plane(slot):
        return pl.ds(pl.multiple_of(line.slots[slot] * per_z * tokens, per_z * tokens), per_z * tokens)

    def save(slot):
        return pltpu.make_async_copy(first.at[plane(slot)], first_out.at[plane(slot)], first_sems.at[slot])

    def project(slot):
        z = line.slots[slot]

        def one(i, _):
            normed, _ = normalize(xbuf[z, i // 2, i % 2].astype(F32))
            low = (normed * prm[G1 : G1 + 1, :] + prm[C1 : C1 + 1, :]).astype(BF16)
            first[pl.ds(pl.multiple_of((z * per_z + i) * tokens, tokens), tokens), :] = low
            return 0

        lax.fori_loop(0, per_z, one, 0)
        at = plane(slot)
        weights = wq_all[...]
        qkv = (dot(first[at, :], weights) + bias[...]).astype(BF16)
        a_ref[at, :] = qkv[:, :128]
        b_ref[at, :] = qkv[:, 128:]
        save(slot).start()

    xg.z_step(1)
    xg.y_step(2)
    xg.core_wait(3)
    project(3)
    xg.z_step(2)
    xg.y_step(1)
    xg.core_wait(2)
    project(2)
    xg.y_step(0)
    dyg.start()
    xg.core_wait(1)
    project(1)
    xg.core_wait(0)
    project(0)
    dyg.step(0)

    length = b_ref.shape[0]
    kc = min(1024, length)
    half = tokens // 2
    if r > 1:
        packed[...] = jnp.zeros_like(packed)

    def per_queries(lb, _):
        gq = lb * r + part
        qs = pl.ds(pl.multiple_of(gq * QB, QB), QB)
        a = a_ref[qs, :] * 0.125
        ids = idcol[qs, :]
        acc[...] = jnp.zeros_like(acc)
        tot[...] = jnp.zeros_like(tot)

        def per_keys(kb, _):
            ks = pl.ds(pl.multiple_of(kb * kc, kc), kc)
            b = b_ref[ks, :]
            s = dot(a, b, NT)
            w = jnp.where(idrow[:, ks] <= ids, jnp.exp(s), 0.0)
            t = w[:, :128]
            for i in range(1, kc // 128):
                t = t + w[:, i * 128 : (i + 1) * 128]
            tot[...] += t
            acc[...] += dot(w.astype(BF16), b)
            return 0

        lax.fori_loop(0, jnp.minimum(((gq + 2) * QB + kc - 1) // kc, length // kc), per_keys, 0)
        t = jnp.sum(tot[...], axis=-1, keepdims=True)
        o = acc[...] / t
        lane = lax.broadcasted_iota(jnp.int32, (QB, 128), 1)
        o_ref[pl.ds(pl.multiple_of(lb * QB, QB), QB), :] = jnp.where(lane < 64, t, o)
        lane = lax.broadcasted_iota(jnp.int32, (half, 128), 1)
        for i in range(QB // tokens):
            lo, hi = o[i * tokens : i * tokens + half], o[i * tokens + half : (i + 1) * tokens]
            packed[gq * (QB // tokens) + i] = jnp.where(lane < 64, pltpu.roll(lo, 64, 1), hi).astype(BF16)
        return 0

    blocks = length // QB // r
    cuts = [0, blocks // 2, blocks * 3 // 4, blocks]
    for k in range(3):
        lax.fori_loop(cuts[k], cuts[k + 1], per_queries, 0)
        if k + 1 < dyg.links:
            dyg.step(k + 1)
    out = ToAll(n_dp, n, lambda f: packed.at[f], att, att_sems, True)
    att[me] = packed[me]
    out.start()
    for k in range(3, dyg.links):
        dyg.step(k)
    out.wait_recv()
    dyg.core_wait()
    for slot in range(4):
        save(slot).wait()
    small.wait_send()
    out.wait_send()
    xg.finish()
    dyg.finish()


def front(n_dp, n, r, x, small, dy, weights):
    tokens, width = x.shape
    count, length = n_dp * n, n * tokens
    cube = cube_plan(n, tokens)
    shape = jax.ShapeDtypeStruct
    vm, hbm = pl.BlockSpec(memory_space=pltpu.VMEM), pl.BlockSpec(memory_space=pl.ANY)
    outs = [
        (shape((count, 16, 128), BF16), vm), (shape((length, width), BF16), hbm), (shape((length, 128), BF16), vm),
        (shape((length, 128), BF16), vm), (shape((length // r, 128), F32), vm), (shape((n, tokens // 2, 128), BF16), vm),
        (shape((2,) * len(cube[0]) + (tokens, width), BF16), hbm),
    ]
    sems = LineGather.sems(n) + [DMA((count,))] * 2 + Gather.sems(cube) + [DMA((n,))] * 2
    ins = [x, *small, dy]
    ins += [weights]
    return pl.pallas_call(
        functools.partial(front_kernel, n_dp, n, r, cube),
        out_shape=[o for o, _ in outs],
        in_specs=[vm] * len(ins),
        out_specs=[s for _, s in outs],
        scratch_shapes=[
            pltpu.VMEM((4, n // 8, 2, tokens, width), BF16), pltpu.VMEM((length, width), BF16), pltpu.VMEM((16, width), F32),
            pltpu.VMEM((2 * width // 128, 128), F32), pltpu.VMEM((1, 256), F32), pltpu.VMEM((1, length), F32),
            pltpu.VMEM((length, 1), F32), pltpu.VMEM((n, tokens // 2, 128), BF16), pltpu.VMEM((QB, 128), F32),
            pltpu.VMEM((QB, 128), F32), DMA((3,)), DMA((4,)),
            pltpu.VMEM((16, 128), F32), pltpu.VMEM((16, 128), BF16),
        ] + sems,
        compiler_params=pltpu.CompilerParams(collective_id=1, has_side_effects=True, vmem_limit_bytes=VMEM_LIMIT),
        name="front",
    )(*ins)


def gelu_both(u):
    c = math.sqrt(2.0 / math.pi)
    t = jnp.tanh(c * (u + 0.044715 * (u * u * u)))
    half = 0.5 * (1.0 + t)
    return u * half, half + 0.5 * u * (1.0 - t * t) * (c * (1.0 + 3.0 * 0.044715 * (u * u)))


def normalize_back(grad, normed, rstd):
    return rstd * (
        grad
        - jnp.mean(grad, axis=-1, keepdims=True)
        - normed * jnp.mean(grad * normed, axis=-1, keepdims=True)
    )


def ffn_kernel(n, r, plan, *refs):
    refs = list(refs)
    take = lambda k: [refs.pop(0) for _ in range(k)]
    att, x_ref, dy_own, dy_hbm, wo_ref, wf_ref, wp_in, bf_ref, par_ref = take(9)
    middle_ref, mg_ref, low_ref, branch_ref, agb, sums_ref, out_hbm, wp_grad, wf_grad, bf_grad = take(10)
    links = len(plan[0]) - 1
    sbuf, dy_ref, grads, act, hid, acc, out_ref, sg, copy_sems, out_sems = take(10)
    bufs, gather_sems, scatter_sems = take(links + 1), take(4), take(4)
    g = Gather(plan, sbuf, gather_sems)
    s = Scatter(plan, acc, bufs, scatter_sems)
    peers = g.peers()
    hello = Greet(1, n, peers)
    wp_ref = wp_in
    dy_copy = pltpu.make_async_copy(dy_hbm, dy_ref, copy_sems)
    dy_copy.start()
    tokens, width = x_ref.shape
    half = tokens // 2
    quarter = (1 << (links - 1)) * tokens
    inner = (slice(None),) * (links - 1)
    core = g.mine[-1]

    lane = lax.broadcasted_iota(jnp.int32, (half, 128), 1)

    def block(h):
        total = att[h * r].astype(F32)
        for i in range(1, r):
            total = total + att[h * r + i].astype(F32)
        return total

    for h in range(0, HEADS, 2):
        b0, b1 = block(h), block(h + 1)
        at = slice(h * 64, h * 64 + 128)
        low_ref[:half, at] = jnp.where(lane < 64, b0, pltpu.roll(b1, 64, 1)).astype(BF16)
        low_ref[half:, at] = jnp.where(lane < 64, pltpu.roll(b0, 64, 1), b1).astype(BF16)
    middle = x_ref[...].astype(F32) + dot(low_ref[...], wo_ref[...]) + par_ref[0:1, :]
    middle_ref[...] = middle
    n2, _ = normalize(middle)
    sbuf[g.own()] = (n2 * par_ref[1:2, :] + par_ref[2:3, :]).astype(BF16)
    hello.wait()
    g.start()
    dy_copy.wait()
    def rows(c, a):
        return pl.ds(pl.multiple_of((2 * c + a) * quarter, quarter), quarter)

    def grad_part(i):
        dy = dy_ref[(i // 2, i % 2) + inner].reshape(quarter, width)
        grads[rows(i // 2, i % 2), :] = dot(dy, wp_ref[...], NT)

    for k in range(links):
        g.step(k)
        if k == 1:
            for i in range(4):
                grad_part(i)
    g.core_wait()
    bf_grad[...] = jnp.zeros_like(bf_grad)

    def hidden_part(c, a):
        at = rows(c, a)
        low = sbuf[(c, a) + inner].reshape(quarter, width)
        active, slope = gelu_both(dot(low, wf_ref[...]) + bf_ref[...])
        act[at, :] = active.astype(BF16)
        h = (slope * grads[at, :]).astype(BF16)
        hid[at, :] = h
        bf_grad[...] += jnp.sum(h.astype(F32), axis=0, keepdims=True)
        acc[(c, a) + inner] = dot(h, wf_ref[...], NT).astype(BF16).reshape((2,) * (links - 1) + (tokens, width))

    for a in range(2):
        hidden_part(1 - core, a)
        s.core(a).start()
    for a in range(2):
        hidden_part(core, a)
        s.add_core(a)
    s.start_links()

    def weight_grads(k):
        at = slice(k * 256, (k + 1) * 256)
        low = sbuf[..., at].reshape(4 * quarter, 256)
        wf_grad[at, :] = jnp.transpose(dot(hid[...], low, TN)).astype(BF16)
        dy = dy_ref[..., at].reshape(4 * quarter, 256)
        wp_grad[:, at] = dot(act[...], dy, TN).astype(BF16)

    def out_part(i):
        at = (i // 2, i % 2) + inner
        if i >= out_ref.shape[0]:
            out_copy(i - out_ref.shape[0]).wait()
        terms = dot(act[rows(i // 2, i % 2), :], wp_ref[...]).astype(BF16)
        out_ref[i % out_ref.shape[0]] = terms.reshape((2,) * (links - 1) + (tokens, width))
        out_copy(i).start()

    def out_copy(i):
        slot = i % out_ref.shape[0]
        return pltpu.make_async_copy(out_ref.at[slot], out_hbm.at[(i // 2, i % 2) + inner], out_sems.at[slot])

    for i in range(4):
        out_part(i)
    for k in range(links):
        s.step(k, sg)
        if k < 2:
            weight_grads(2 * k)
            weight_grads(2 * k + 1)

    second_grad = sg[...]
    dy = dy_own[...].astype(F32)
    n2, rstd2 = normalize(middle_ref[...])
    mg = dy + normalize_back(second_grad * par_ref[1:2, :], n2, rstd2)
    mg_ref[...] = mg
    branch = mg.astype(BF16)
    branch_ref[...] = branch
    grad = dot(branch, wo_ref[...], NT)
    for h in range(0, HEADS, 2):
        lo, hi = grad[:half, h * 64 : h * 64 + 128], grad[half:, h * 64 : h * 64 + 128]
        b0 = jnp.where(lane < 64, lo, pltpu.roll(hi, 64, 1)).astype(BF16)
        b1 = jnp.where(lane < 64, pltpu.roll(lo, 64, 1), hi).astype(BF16)
        for i in range(r):
            agb[h * r + i] = b0
            agb[(h + 1) * r + i] = b1
    column = lambda v: jnp.sum(v, axis=0, keepdims=True)
    sums_ref[0:1, :] = column(branch.astype(F32))
    sums_ref[1:2, :] = column(second_grad * n2)
    sums_ref[2:3, :] = column(second_grad)
    sums_ref[3:4, :] = column(dy)
    for i in range(4 - out_ref.shape[0], 4):
        out_copy(i).wait()
    s.finish()
    g.finish()


def ffn(n, r, att, x, dy, dy_all, wo, wf, wp, bf, params):
    tokens, width = x.shape
    units = wf.shape[1]
    plan = cube_plan(n, tokens)
    block = (2,) * len(plan[0])
    length = n * tokens
    shape = jax.ShapeDtypeStruct
    vm, hbm = pl.BlockSpec(memory_space=pltpu.VMEM), pl.BlockSpec(memory_space=pl.ANY)
    return pl.pallas_call(
        functools.partial(ffn_kernel, n, r, plan),
        out_shape=[
            shape((tokens, width), F32), shape((tokens, width), F32), shape((tokens, width), BF16), shape((tokens, width), BF16),
            shape((n, tokens // 2, 128), BF16), shape((4, width), F32), shape(block + (tokens, width), BF16),
            shape((units, width), BF16), shape((width, units), BF16), shape((1, units), F32),
        ],
        in_specs=[vm, vm, vm, hbm, vm, vm, vm, vm, vm],
        out_specs=[vm, vm, vm, vm, vm, vm, hbm, vm, vm, vm],
        scratch_shapes=[
            pltpu.VMEM(block + (tokens, width), BF16), pltpu.VMEM(block + (tokens, width), BF16), pltpu.VMEM((length, units), F32),
            pltpu.VMEM((length, units), BF16), pltpu.VMEM((length, units), BF16), pltpu.VMEM(block + (tokens, width), BF16),
            pltpu.VMEM((2,) + block[2:] + (tokens, width), BF16), pltpu.VMEM((tokens, width), F32), DMA, DMA((2,)),
        ] + Scatter.scratch(plan, tokens, width) + Gather.sems(plan) + Scatter.sems(plan),
        compiler_params=pltpu.CompilerParams(collective_id=2, has_side_effects=True, vmem_limit_bytes=VMEM_LIMIT),
        name="ffn",
    )(att, x, dy, dy_all, wo, wf, wp, bf, params)


def project_rows(rows, prm):
    normed, _ = normalize(rows.astype(F32))
    return (normed * prm[G1 : G1 + 1, :] + prm[C1 : C1 + 1, :]).astype(BF16)


def lead_kernel(n_dp, n, cube, whole, *refs):
    refs = list(refs)
    take = lambda k: [refs.pop(0) for _ in range(k)]
    x_ref, pieces, (dy_own, w_qkv, w_fc, w_proj, w_out) = refs.pop(0), take(9), take(5)
    small_all, first_out, a_ref, b_ref, o_ref, wq_all, par_ref = take(7)
    middle_ref, mg_ref, low_ref, branch_ref, agb, sums_ref, out_hbm, wp_grad, wf_grad, bf_grad = take(10)
    xbuf, first, prm, bqv, bias, bf_row, idrow, idcol, packed, acc, tot, att, wqb, wfb = take(14)
    wf_all, wo_all, wp_ref, dy_ref, sbuf, grads, act, hid, terms, out_ref, sg = take(11)
    first_sems, out_sems, tile, small_ref = take(4)
    links = len(cube[0]) - 1
    bufs = take(links + 1)
    line_sems, small_sems, dy_sems, att_sems, wq_sems, wf_sems, wo_sems = take(6), take(2), take(4), take(2), take(4), take(2), take(4)
    wp_sems, gather_sems, scatter_sems = take(2), take(4), take(4)

    tokens, width = x_ref.shape
    length = n * tokens
    rows, units = w_fc.shape[0], w_proj.shape[0]
    count = n_dp * n
    d, me = lax.axis_index("dp"), lax.axis_index("ctx")
    flat = d * n + me
    rank, group = group_of(n, flat)
    line = Line(n)
    hello = Greet(n_dp, n)

    xg = LineGather(line, xbuf, line_sems)
    small = ToAll(n_dp, n, lambda f: small_ref, small_all, small_sems)
    wq = ToAll(n_dp, n, lambda f: wqb.at[f], wq_all.at[d], wq_sems[:2], True)
    wf = ToAll(n_dp, n, lambda f: wfb.at[group_of(n, f)[0]], wf_all, wf_sems)
    dyg = Gather(cube, dy_ref, dy_sems)
    wog = Gather(whole, wo_all, wo_sems)
    out = ToAll(n_dp, n, lambda f: packed.at[f], att, att_sems, True)
    g = Gather(cube, sbuf, gather_sems)
    s = Scatter(cube, terms, bufs, scatter_sems)
    dps, wps = [], []
    for i in range(1, n_dp):
        dps.append(remote(wq_all.at[d], wq_all.at[d], wq_sems[2].at[i], wq_sems[3].at[i], {"dp": (d + i) % n_dp}))
        to = wp_ref.at[pl.ds(pl.multiple_of(group * units, units), units)]
        wps.append(remote(w_proj, to, wp_sems[0].at[i], wp_sems[1].at[i], group_peer(n, i, n_dp)[1]))

    low = lax.broadcasted_iota(jnp.int32, (rows, 128), 1) < 64
    for h in range(0, HEADS, 2):
        q, k, v = (w_qkv[:, p * width + h * 64 : p * width + h * 64 + 128].astype(F32) for p in range(3))
        turn = lambda t: pltpu.roll(t, 64, 1)
        wqb[h, :, :128] = jnp.where(low, q, 0.0).astype(BF16)
        wqb[h, :, 128:] = jnp.where(low, k, turn(v)).astype(BF16)
        wqb[h + 1, :, :128] = jnp.where(low, turn(q), 0.0).astype(BF16)
        wqb[h + 1, :, 128:] = jnp.where(low, turn(k), v).astype(BF16)
    xbuf[line.z, line.y, line.c] = x_ref[...]
    put_small(pieces, tile, small_ref)
    small_all[flat] = small_ref[...]
    wq_all[d, me] = wqb[me]
    wo_all[wog.own()] = w_out[...]
    hello.wait()
    xg.start()
    small.start()
    wq.start()
    wog.start()
    for m in range(n):
        for i in range(n_dp):
            at = ((i // 2 * 2 + m // (n // 2)) * n + i % 2 * (n // 2) + m % (n // 2)) * units
            wfb[m, :, i * units : (i + 1) * units] = w_fc[:, at : at + units]
    dy_ref[dyg.own()] = dy_own[...]
    wf_all[flat] = wfb[rank]
    wp_ref[pl.ds(pl.multiple_of(group * units, units), units), :] = w_proj[...]
    xg.z_step(0)
    xg.y_step(3)
    wq.wait_recv()
    for c in dps:
        c.start()
    small.wait_recv()
    put_params(count, width, small_all, prm, bqv)
    odd = me % 2
    bias[:, :128] = half_row(bqv[pl.ds(me // 2, 1), :], odd, False)
    bias[:, 128:] = half_row(bqv[pl.ds(width // 128 + me // 2, 1), :], odd, True)
    for i in range(n_dp):
        owner = (i // 2 * 2 + d % 2) * n + i % 2 * (n // 2) + me % (n // 2)
        bf_row[:, i * units : (i + 1) * units] = small_all[owner].astype(F32)[BF : BF + 1, :units]
    par_ref[0:1, :] = prm[G1 : G1 + 1, :]
    par_ref[1:2, :] = prm[BP : BP + 1, :]
    put_ids(n, small_all, d * n, idrow, idcol)
    per_z = n // 4

    def plane(slot):
        return pl.ds(pl.multiple_of(line.slots[slot] * per_z * tokens, per_z * tokens), per_z * tokens)

    def save(slot):
        return pltpu.make_async_copy(first.at[plane(slot)], first_out.at[plane(slot)], first_sems.at[slot])

    def project(slot):
        z = line.slots[slot]

        def one(i, _):
            at = pl.ds(pl.multiple_of((z * per_z + i) * tokens, tokens), tokens)
            first[at, :] = project_rows(xbuf[z, i // 2, i % 2], prm)
            return 0

        lax.fori_loop(0, per_z, one, 0)
        at = plane(slot)
        qkv = (dot(first[at, :], wq_all[...].reshape(width, 256)) + bias[...]).astype(BF16)
        a_ref[at, :] = qkv[:, :128]
        b_ref[at, :] = qkv[:, 128:]
        save(slot).start()

    xg.z_step(1)
    xg.y_step(2)
    wog.step(0)
    for c in dps:
        c.wait_recv()
    xg.core_wait(3)
    project(3)
    xg.z_step(2)
    xg.y_step(1)
    wog.step(1)
    xg.core_wait(2)
    project(2)
    xg.y_step(0)
    dyg.start()
    for c in wps:
        c.start()
    wf.start()
    wog.step(2)
    xg.core_wait(1)
    project(1)
    xg.core_wait(0)
    project(0)
    dyg.step(0)

    kc = min(1024, length)
    half = tokens // 2
    lane = lax.broadcasted_iota(jnp.int32, (half, 128), 1)

    def per_queries(gq, _):
        qs = pl.ds(pl.multiple_of(gq * QB, QB), QB)
        a = a_ref[qs, :] * 0.125
        ids = idcol[qs, :]
        acc[...] = jnp.zeros_like(acc)
        tot[...] = jnp.zeros_like(tot)

        def per_keys(kb, _):
            ks = pl.ds(pl.multiple_of(kb * kc, kc), kc)
            b = b_ref[ks, :]
            w = jnp.where(idrow[:, ks] <= ids, jnp.exp(dot(a, b, NT)), 0.0)
            t = w[:, :128]
            for i in range(1, kc // 128):
                t = t + w[:, i * 128 : (i + 1) * 128]
            tot[...] += t
            acc[...] += dot(w.astype(BF16), b)
            return 0

        lax.fori_loop(0, jnp.minimum(((gq + 2) * QB + kc - 1) // kc, length // kc), per_keys, 0)
        t = jnp.sum(tot[...], axis=-1, keepdims=True)
        o = acc[...] / t
        o_ref[qs, :] = jnp.where(lax.broadcasted_iota(jnp.int32, (QB, 128), 1) < 64, t, o)
        for i in range(QB // tokens):
            lo, hi = o[i * tokens : i * tokens + half], o[i * tokens + half : (i + 1) * tokens]
            packed[gq * (QB // tokens) + i] = jnp.where(lane < 64, pltpu.roll(lo, 64, 1), hi).astype(BF16)
        return 0

    blocks = length // QB
    lax.fori_loop(0, blocks // 2, per_queries, 0)
    dyg.step(1)
    wog.step(3)
    lax.fori_loop(blocks // 2, blocks, per_queries, 0)
    att[me] = packed[me]
    out.start()
    for k in range(4, wog.links):
        wog.step(k)
    wog.core_wait()
    out.wait_recv()

    for h in range(0, HEADS, 2):
        b0, b1 = att[h].astype(F32), att[h + 1].astype(F32)
        at = slice(h * 64, h * 64 + 128)
        low_ref[:half, at] = jnp.where(lane < 64, b0, pltpu.roll(b1, 64, 1)).astype(BF16)
        low_ref[half:, at] = jnp.where(lane < 64, pltpu.roll(b0, 64, 1), b1).astype(BF16)
    middle = x_ref[...].astype(F32) + dot(low_ref[...], wo_all[...].reshape(width, width)) + prm[BO : BO + 1, :]
    middle_ref[...] = middle
    n2, _ = normalize(middle)
    sbuf[g.own()] = (n2 * prm[G2 : G2 + 1, :] + prm[C2 : C2 + 1, :]).astype(BF16)
    g.start()
    for k in range(2, links):
        dyg.step(k)
    for c in wps:
        c.wait_recv()
    dyg.core_wait()

    quarter = (1 << (links - 1)) * tokens
    inner = (slice(None),) * (links - 1)
    block = (2,) * (links - 1) + (tokens, width)
    core = g.mine[-1]

    def span(c, a):
        return pl.ds(pl.multiple_of((2 * c + a) * quarter, quarter), quarter)

    def grad_part(i):
        dy = dy_ref[(i // 2, i % 2) + inner].reshape(quarter, width)
        grads[span(i // 2, i % 2), :] = dot(dy, wp_ref[...], NT)

    for k in range(links):
        grad_part(k)
        g.step(k)
    for k in range(links, 4):
        grad_part(k)
    wf.wait_recv()
    g.core_wait()
    bf_grad[...] = jnp.zeros_like(bf_grad)

    def hidden_part(c, a):
        at = span(c, a)
        weights = wf_all[...].reshape(width, -1)
        active, slope = gelu_both(dot(sbuf[(c, a) + inner].reshape(quarter, width), weights) + bf_row[...])
        act[at, :] = active.astype(BF16)
        h = (slope * grads[at, :]).astype(BF16)
        hid[at, :] = h
        bf_grad[...] += jnp.sum(h.astype(F32), axis=0, keepdims=True)
        terms[(c, a) + inner] = dot(h, weights, NT).astype(BF16).reshape(block)

    for a in range(2):
        hidden_part(1 - core, a)
        s.core(a).start()
    for a in range(2):
        hidden_part(core, a)
        s.add_core(a)
    s.start_links()

    def weight_grads(k):
        at = slice(k * 256, (k + 1) * 256)
        low = sbuf[..., at].reshape(4 * quarter, 256)
        wf_grad[at, :] = jnp.transpose(dot(hid[...], low, TN)).astype(BF16)
        wp_grad[:, at] = dot(act[...], dy_ref[..., at].reshape(4 * quarter, 256), TN).astype(BF16)

    def out_copy(i):
        return pltpu.make_async_copy(out_ref.at[i % 2], out_hbm.at[(i // 2, i % 2) + inner], out_sems.at[i % 2])

    for i in range(4):
        if i >= 2:
            out_copy(i - 2).wait()
        out_ref[i % 2] = dot(act[span(i // 2, i % 2), :], wp_ref[...]).astype(BF16).reshape(block)
        out_copy(i).start()
    for k in range(links):
        s.step(k, sg)
        if k < 2:
            weight_grads(2 * k)
            weight_grads(2 * k + 1)

    second_grad = sg[...]
    dy = dy_own[...].astype(F32)
    n2, rstd2 = normalize(middle_ref[...])
    mg = dy + normalize_back(second_grad * prm[G2 : G2 + 1, :], n2, rstd2)
    mg_ref[...] = mg
    branch = mg.astype(BF16)
    branch_ref[...] = branch
    grad = dot(branch, wo_all[...].reshape(width, width), NT)
    for h in range(0, HEADS, 2):
        lo, hi = grad[:half, h * 64 : h * 64 + 128], grad[half:, h * 64 : h * 64 + 128]
        agb[h] = jnp.where(lane < 64, lo, pltpu.roll(hi, 64, 1)).astype(BF16)
        agb[h + 1] = jnp.where(lane < 64, pltpu.roll(lo, 64, 1), hi).astype(BF16)
    column = lambda v: jnp.sum(v, axis=0, keepdims=True)
    sums_ref[0:1, :] = column(branch.astype(F32))
    sums_ref[1:2, :] = column(second_grad * n2)
    sums_ref[2:3, :] = column(second_grad)
    sums_ref[3:4, :] = column(dy)
    for i in (2, 3):
        out_copy(i).wait()
    for slot in range(4):
        save(slot).wait()
    for c in (wq, wf, small, out):
        c.wait_send()
    for c in dps + wps:
        c.wait_send()
    for c in (xg, wog, dyg, g, s):
        c.finish()


def lead(n_dp, n, x, small, dy, w_qkv, w_fc, w_proj, w_out):
    tokens, width = x.shape
    count, length = n_dp * n, n * tokens
    rows, units = w_fc.shape[0], n_dp * w_proj.shape[0]
    cube, whole = cube_plan(n, tokens), all_plan(n_dp, n, rows)
    block = (2,) * len(cube[0]) + (tokens, width)
    shape = jax.ShapeDtypeStruct
    vm, hbm = pl.BlockSpec(memory_space=pltpu.VMEM), pl.BlockSpec(memory_space=pl.ANY)
    outs = [
        (shape((count, 16, 128), BF16), vm), (shape((length, width), BF16), hbm), (shape((length, 128), BF16), vm),
        (shape((length, 128), BF16), vm), (shape((length, 128), F32), vm), (shape((n_dp, n, rows, 256), BF16), vm),
        (shape((2, width), F32), vm), (shape((tokens, width), F32), vm), (shape((tokens, width), F32), vm),
        (shape((tokens, width), BF16), vm), (shape((tokens, width), BF16), vm), (shape((n, tokens // 2, 128), BF16), vm),
        (shape((4, width), F32), vm), (shape(block, BF16), hbm), (shape((units, width), BF16), vm),
        (shape((width, units), BF16), vm), (shape((1, units), F32), vm),
    ]
    return pl.pallas_call(
        functools.partial(lead_kernel, n_dp, n, cube, whole),
        out_shape=[o for o, _ in outs],
        in_specs=[vm] * 15,
        out_specs=[s for _, s in outs],
        scratch_shapes=[
            pltpu.VMEM((4, n // 8, 2, tokens, width), BF16), pltpu.VMEM((length, width), BF16), pltpu.VMEM((16, width), F32),
            pltpu.VMEM((2 * width // 128, 128), F32), pltpu.VMEM((1, 256), F32), pltpu.VMEM((1, units), F32),
            pltpu.VMEM((1, length), F32), pltpu.VMEM((length, 1), F32), pltpu.VMEM((n, tokens // 2, 128), BF16),
            pltpu.VMEM((QB, 128), F32), pltpu.VMEM((QB, 128), F32), pltpu.VMEM((n, tokens // 2, 128), BF16),
            pltpu.VMEM((n, rows, 256), BF16), pltpu.VMEM((n, rows, units), BF16),
            pltpu.VMEM((count, rows, units), BF16), pltpu.VMEM((2,) * len(whole[0]) + (rows, width), BF16),
            pltpu.VMEM((units, width), BF16), pltpu.VMEM(block, BF16), pltpu.VMEM(block, BF16),
            pltpu.VMEM((length, units), F32), pltpu.VMEM((length, units), BF16), pltpu.VMEM((length, units), BF16),
            pltpu.VMEM(block, BF16), pltpu.VMEM((2,) + block[2:], BF16), pltpu.VMEM((tokens, width), F32), DMA((4,)), DMA((2,)),
            pltpu.VMEM((16, 128), F32), pltpu.VMEM((16, 128), BF16),
        ] + Scatter.scratch(cube, tokens, width) + LineGather.sems(n) + [DMA((count,))] * 2 + Gather.sems(cube) + [DMA((n,))] * 2
        + [DMA((n,))] * 2 + [DMA((n_dp,))] * 2 + [DMA((count,))] * 2 + Gather.sems(whole) + [DMA((n_dp,))] * 2
        + Gather.sems(cube) + Scatter.sems(cube),
        compiler_params=pltpu.CompilerParams(collective_id=1, has_side_effects=True, vmem_limit_bytes=VMEM_LIMIT),
        name="lead",
    )(x, *small, dy, w_qkv, w_fc, w_proj, w_out)


def back_kernel(n_dp, n, r, spread, cube, whole, *refs):
    refs = list(refs)
    take = lambda k: [refs.pop(0) for _ in range(k)]
    agb, a_ref, b_ref, o_ref, small_all, wq_ref, first, part_out, x_ref, mid_ref, mg_ref, par_ref, sums_in, bf_grad = take(14)
    if spread:
        low_ref, branch_ref, wfg, wpg = take(4)
    out_ref, ig_ref, sums = take(3)
    if spread:
        wq_got, wf_got, wp_got, wo_own = take(4)
    else:
        (wq_sum,) = take(1)
    ag, idrow, idcol, mixed, dqacc, dkv, acc, kbuf, ybuf, zbuf, fg, got, msg, columns, column_sem, own_out, own_sem, osum = take(18)
    links = len(cube[0]) - 1
    out_bufs = take(links + 1)
    if r > 1:
        (dkv_got,) = take(1)
        pair_sems = take(2)
    ag_sems, line_sems, out_sems, msg_sems = take(2), take(6), take(4), take(2)
    if spread:
        wq_part, wq_mine, wq_else, wo_part = take(4)
        wq_sems, wf_sems, wp_sems = take(4), take(2), take(2)
        wo_bufs = take(len(whole[0]))
        wo_sems = take(4)

    tokens, width = x_ref.shape
    length = b_ref.shape[0]
    count = n_dp * n
    d, me = lax.axis_index("dp"), lax.axis_index("ctx")
    flat = d * n + me
    head, part = me // r, me % r
    line = Line(n)
    hello = Greet(n_dp, n)
    kc = min(1024, length)
    half = tokens // 2

    grads = ToAll(n_dp, n, lambda f: agb.at[f], ag, ag_sems, True)
    outs = Scatter(cube, part_out, out_bufs, out_sems, own_out)
    own_copy = outs.fetch_own(own_sem)
    own_copy.start()
    ag[me] = agb[me]
    if spread:
        wf = ToAll(n_dp, n, lambda f: wfg.at[f], wf_got, wf_sems)
        wq = ToAll(n_dp, n, lambda f: wq_mine.at[f], wq_got, wq_sems[:2], True)
        wo = Scatter(whole, wo_part, wo_bufs, wo_sems)
        wf_got[flat] = wfg[flat]
        rank, group = group_of(n, flat)
        wp_got[group] = wpg[group]
        wps, dps = [], []
        for i in range(1, n_dp):
            g, peer = group_peer(n, i, n_dp)
            wps.append(remote(wpg.at[g], wp_got.at[group], wp_sems[0].at[i], wp_sems[1].at[i], peer))
            dps.append(remote(wq_part.at[(d + i) % n_dp], wq_else.at[i], wq_sems[2].at[i], wq_sems[3].at[i], {"dp": (d + i) % n_dp}))
    else:
        rank, group = group_of(n, flat)
    dkv[...] = jnp.zeros_like(dkv)
    if r > 1:
        mixed[...] = jnp.zeros_like(mixed)
    hello.wait()
    grads.start()
    for h in range(2):
        outs.core(h).start()
    if spread:
        for c in wps:
            c.start()
    put_ids(n, small_all, d * n, idrow, idcol)
    if spread:
        rows = width // count
        for k in range(width // 256):
            terms = dot(low_ref[:, k * 256 : (k + 1) * 256], branch_ref[...], TN).astype(BF16)
            for i in range(256 // rows):
                f = k * (256 // rows) + i
                bits = tuple((f >> b) & 1 for b in range(len(whole[0]) - 1, -1, -1))
                wo_part[bits] = terms[i * rows : (i + 1) * rows]
        for h in range(2):
            wo.core(h).start()
    own_copy.wait()
    for h in range(2):
        outs.add_core(h)
    outs.start_links()
    grads.wait_recv()
    if spread:
        wf.start()

    def per_queries(lb, _):
        gq = lb * r + part
        qs = pl.ds(pl.multiple_of(gq * QB, QB), QB)
        at = pl.ds(pl.multiple_of(lb * QB, QB), QB)
        lane = lax.broadcasted_iota(jnp.int32, (half, 128), 1)
        pieces = []
        for i in range(QB // tokens):
            block = ag[gq * (QB // tokens) + i].astype(F32)
            pieces += [jnp.where(lane >= 64, pltpu.roll(block, 64, 1), 0.0), jnp.where(lane >= 64, block, 0.0)]
        grad = jnp.concatenate(pieces, axis=0)
        o = o_ref[at, :]
        inverse = 1.0 / o[:, :1]
        upper = lax.broadcasted_iota(jnp.int32, (QB, 128), 1) >= 64
        ratio = jnp.sum(jnp.where(upper, grad * o, 0.0), axis=-1, keepdims=True) * inverse
        ratio = jnp.transpose(jnp.broadcast_to(ratio, (QB, 128)))[:1, :]
        do = (grad * inverse).astype(BF16)
        a = a_ref[qs, :]
        scaled = a * 0.125
        ado = jnp.concatenate([a, do], axis=0)
        ids = idrow[:, qs]
        dqacc[...] = jnp.zeros_like(dqacc)

        def per_keys(kb, _):
            ks = pl.ds(pl.multiple_of(kb * kc, kc), kc)
            b = b_ref[ks, :]
            w = jnp.where(idcol[ks, :] <= ids, jnp.exp(dot(b, scaled, NT)), 0.0)
            g = (w * (dot(b, do, NT) - ratio)).astype(BF16)
            dkv[ks, :] += dot(jnp.concatenate([g, w.astype(BF16)], axis=1), ado)
            dqacc[...] += dot(g, b, TN)
            return 0

        lax.fori_loop(0, jnp.minimum(((gq + 2) * QB + kc - 1) // kc, length // kc), per_keys, 0)
        mixed[qs, :128] = jnp.where(upper, 0.0, dqacc[...] * 0.125).astype(BF16)
        return 0

    blocks = length // QB // r
    cuts = [0, blocks // 2, blocks * 3 // 4, blocks]
    for k in range(3):
        lax.fori_loop(cuts[k], cuts[k + 1], per_queries, 0)
        if k + 1 < links:
            outs.step(k, osum)
    if spread:
        for h in range(2):
            wo.add_core(h)

    def fetch(k):
        return pltpu.make_async_copy(first.at[:, pl.ds(pl.multiple_of(k * 256, 256), 256)], columns, column_sem)

    turns = [((d + 1) * (width // 256 // n_dp) + i) % (width // 256) if spread else i for i in range(width // 256)]
    fetch(turns[0]).start()
    low = lax.broadcasted_iota(jnp.int32, (length, 128), 1) < 64
    total = dkv[...]
    if r > 1:
        both = remote(dkv, dkv_got, pair_sems[0], pair_sems[1], line.core)
        both.start()
        both.wait()
        total = jnp.where(part == 0, total + dkv_got[...], 0.0)
    mixed[:, 128:] = jnp.where(low, total * 0.125, total).astype(BF16)

    rs = LineScatter(line, acc, kbuf, ybuf, zbuf, line_sems)
    per_z = n // 4 * tokens

    def first_grad(slot):
        z = line.slots[slot]
        at = pl.ds(pl.multiple_of(z * per_z, per_z), per_z)
        acc[z] = dot(mixed[at, :], wq_ref[...], NT).astype(BF16).reshape(n // 8, 2, tokens, width)
        rs.core_start(slot)

    first_grad(0)
    for slot in range(1, 4):
        first_grad(slot)
        rs.core_step(slot - 1)
    rs.core_step(3)
    for k in range(min(2, links - 1), links):
        outs.step(k, osum)
    if spread:
        wo.start_links()

    def wq_grad(i):
        k = turns[i]
        fetch(k).wait()
        g = jnp.transpose(dot(mixed[...], columns[...], TN))
        if i + 1 < len(turns):
            fetch(turns[i + 1]).start()
        if spread:
            per = n_dp * 256 // width
            q = 256 // rows
            at = k * q
            wq_part[at // n, pl.ds(at % n, q)] = g.astype(BF16).reshape(q, rows, 256)
        else:
            wq_sum[pl.ds(pl.multiple_of(k * 256, 256), 256), :] = g

    ahead = len(turns) - len(turns) // n_dp if spread else 2
    for i in range(ahead):
        wq_grad(i)
    if spread:
        for c in dps:
            c.start()
    rs.z_step(0)
    for i in range(ahead, len(turns)):
        wq_grad(i)
    rs.z_step(1)
    if spread:
        total = wq_part[d].astype(F32)
        for i, c in enumerate(dps):
            c.wait_recv()
            total = total + wq_else[i + 1].astype(F32)
        wq_mine[...] = total.astype(BF16)
        wq_got[me] = wq_mine[me]
        wq.start()
        wo.step(0, wo_own)
    column = jnp.sum(mixed[...].astype(F32), axis=0, keepdims=True)
    odd = head % 2
    q_row = half_row(column[:, :128], 0, False)
    q_row = jnp.where(odd == 1, pltpu.roll(q_row, 64, 1), q_row)
    v_row = half_row(column[:, 128:], 1, True)
    v_row = jnp.where(odd == 1, v_row, pltpu.roll(v_row, 64, 1))
    rs.z_step(2)
    out_ref[...] = (mid_ref[...] + osum[...] + par_ref[1:2, :]).astype(BF16)
    n1, rstd1 = normalize(x_ref[...].astype(F32))
    if spread:
        wo.step(1, wo_own)

    wide = bf_grad.shape[1] // 128

    def prepare(f, _):
        tile = f * 2 * width // count // 128
        bqv = jnp.where(tile == head // 2, q_row, 0.0) + jnp.where(tile == width // 128 + head // 2, v_row, 0.0)
        msg[f, 6:7, :] = bqv
        same = group_of(n, f)[0] == rank
        for i in range(wide):
            msg[f, 7 + i : 8 + i, :] = jnp.where(same, bf_grad[:, i * 128 : (i + 1) * 128], 0.0)
        return 0

    msg[...] = jnp.zeros_like(msg)
    lax.fori_loop(0, count, prepare, 0)
    rs.last(fg)

    grad = fg[...]
    gain = jnp.sum(grad * n1, axis=0, keepdims=True)
    shift = jnp.sum(grad, axis=0, keepdims=True)
    per = 128 * count // width
    for k in range(width // 128):
        at = slice(k * 128, (k + 1) * 128)
        lines = jnp.concatenate([gain[:, at], shift[:, at], sums_in[:, at]], axis=0)

        def fill(i, _, k=k, lines=lines):
            msg[k * per + i, 0:6, :] = lines
            return 0

        lax.fori_loop(0, per, fill, 0)
    tell = ToAll(n_dp, n, lambda f: msg.at[f], got, msg_sems)
    tell.start()
    got[flat] = msg[flat]
    ig_ref[...] = (mg_ref[...] + normalize_back(grad * par_ref[0:1, :], n1, rstd1)).astype(BF16)
    if spread:
        for k in range(2, wo.links):
            wo.step(k, wo_own)
        wf.wait_recv()
        wq.wait_recv()
        for c in wps:
            c.wait()
    tell.wait_recv()
    sums[...] = jnp.sum(got[...], axis=0)
    tell.wait_send()
    if spread:
        wf.wait_send()
        wq.wait_send()
        for c in dps:
            c.wait_send()
        wo.finish()
    grads.wait_send()
    outs.finish()
    rs.finish()


def back(n_dp, n, r, agb, a, b, o, small_all, wq, first, part_out, x, middle, mg, params, sums4, bf_grad, grads):
    tokens, width = x.shape
    count, length = n_dp * n, n * tokens
    spread = grads is not None
    cube = cube_plan(n, tokens)
    links = len(cube[0]) - 1
    whole = None
    shape = jax.ShapeDtypeStruct
    ins = [agb, a, b, o, small_all, wq, first, part_out, x, middle, mg, params, sums4, bf_grad]
    outs = [shape((tokens, width), BF16), shape((tokens, width), BF16), shape((16, 128), F32)]
    scratch = [
        pltpu.VMEM((n, tokens // 2, 128), BF16), pltpu.VMEM((1, length), F32), pltpu.VMEM((length, 1), F32),
        pltpu.VMEM((length, 256), BF16), pltpu.VMEM((QB, 128), F32), pltpu.VMEM((length, 128), F32),
        pltpu.VMEM((4, n // 8, 2, tokens, width), BF16),
    ] + LineScatter.scratch(n, tokens, width) + [
        pltpu.VMEM((tokens, width), F32), pltpu.VMEM((count, 16, 128), F32), pltpu.VMEM((count, 16, 128), F32),
        pltpu.VMEM((length, 256), BF16), DMA, pltpu.VMEM((2,) * links + (tokens, width), BF16), DMA,
        pltpu.VMEM((tokens, width), F32),
    ] + Scatter.scratch(cube, tokens, width)
    if r > 1:
        scratch += [pltpu.VMEM((length, 128), F32), DMA, DMA]
    scratch += [DMA((n,))] * 2 + LineScatter.sems(n) + Scatter.sems(cube) + [DMA((count,))] * 2
    if spread:
        low, branch, wfg, wpg = grads
        rows = width // count
        whole = all_plan(n_dp, n, rows)
        ins += [low, branch, wfg, wpg]
        outs += [shape((n, rows, 256), BF16), shape(wfg.shape, BF16), shape(wpg.shape, BF16), shape((rows, width), F32)]
        scratch += [
            pltpu.VMEM((n_dp, n, rows, 256), BF16), pltpu.VMEM((n, rows, 256), BF16), pltpu.VMEM((n_dp, n, rows, 256), BF16),
            pltpu.VMEM((2,) * len(whole[0]) + (rows, width), BF16),
        ]
        scratch += [DMA((n,))] * 2 + [DMA((n_dp,))] * 2 + [DMA((count,))] * 2 + [DMA((n_dp,))] * 2
        scratch += Scatter.scratch(whole, rows, width) + Scatter.sems(whole)
    else:
        outs += [shape((width, 256), F32)]
    vm, hbm = pl.BlockSpec(memory_space=pltpu.VMEM), pl.BlockSpec(memory_space=pl.ANY)
    return pl.pallas_call(
        functools.partial(back_kernel, n_dp, n, r, spread, cube, whole),
        out_shape=outs,
        in_specs=[hbm if v is first or v is part_out else vm for v in ins],
        out_specs=[vm] * len(outs),
        scratch_shapes=scratch,
        compiler_params=pltpu.CompilerParams(collective_id=3, has_side_effects=True, vmem_limit_bytes=VMEM_LIMIT),
        name="back",
    )(*ins)


def own_sums(n_dp, n, piece, sums):
    flat = lax.axis_index("dp") * n + lax.axis_index("ctx")
    wide = pltpu.roll(sums, (128 - flat * piece % 128) % 128, 1)
    return wide, pltpu.roll(sums, (128 - flat * 2 * piece % 128) % 128, 1)[6:7]


def finish_kernel(n_dp, n, out_in, ig_in, sums, wq_got, wf_got, wp_got, wo_in, *outs):
    out, ig, g1, c1, wq_own, bqv, wo_own, bo, g2, c2, wf_own, bf, wp_own, bp = outs
    count = n_dp * n
    rows, width = wo_in.shape
    units = wp_got.shape[1]
    out[0] = out_in[...]
    ig[0] = ig_in[...]
    wo_own[...] = wo_in[...]
    wp_own[...] = jnp.sum(wp_got[...].astype(F32), axis=0)
    for f in range(count):
        m, g = group_of(n, f)
        total = 0.0
        for i in range(n_dp):
            source = (i // 2 * 2 + m // (n // 2)) * n + i % 2 * (n // 2) + m % (n // 2)
            total = total + wf_got[source, :, g * units : (g + 1) * units].astype(F32)
        wf_own[:, f * units : (f + 1) * units] = total
    lower = lax.broadcasted_iota(jnp.int32, (rows, 128), 1) < 64
    turn = lambda t: pltpu.roll(t, 64, 1)
    for h in range(0, HEADS, 2):
        (q0, e0), (q1, e1) = ((wq_got[i, :, :128].astype(F32), wq_got[i, :, 128:].astype(F32)) for i in (h, h + 1))
        for p, v in enumerate((jnp.where(lower, q0, turn(q1)), jnp.where(lower, e0, turn(e1)), jnp.where(lower, turn(e0), e1))):
            wq_own[:, p * width + h * 64 : p * width + h * 64 + 128] = v
    wide, double = own_sums(n_dp, n, rows, sums[...])
    for i, ref in enumerate((g1, c1, bo, g2, c2, bp)):
        ref[...] = wide[i : i + 1, :rows]
    bqv[...] = double[:, : 2 * rows]
    group = group_of(n, lax.axis_index("dp") * n + lax.axis_index("ctx"))[1]
    bf[...] = sums[pl.ds(7 + group, 1), :]


def finish(n_dp, n, out, ig, sums, wq_got, wf_got, wp_got, wo):
    rows, width = wo.shape
    units = wp_got.shape[1]
    shape = jax.ShapeDtypeStruct
    row = shape((1, rows), F32)
    vm = pl.BlockSpec(memory_space=pltpu.VMEM)
    got = pl.pallas_call(
        functools.partial(finish_kernel, n_dp, n),
        out_shape=[
            shape((1,) + out.shape, BF16), shape((1,) + ig.shape, BF16), row, row, shape((rows, 3 * width), F32),
            shape((1, 2 * rows), F32), shape((rows, width), F32), row, row, row, shape((rows, n_dp * n * units), F32),
            shape((1, units), F32), shape((units, width), F32), row,
        ],
        in_specs=[vm] * 7,
        out_specs=[vm] * 14,
        compiler_params=pltpu.CompilerParams(vmem_limit_bytes=VMEM_LIMIT),
        name="finish",
    )(out, ig, sums, wq_got, wf_got, wp_got, wo)
    return tuple(v.reshape(-1) if v.shape[0] == 1 and v.ndim == 2 else v for v in got)


def local(n_dp, n, inputs, cotangent, block_ids, ln1_gain, ln1_bias, w_qkv, b_qkv, w_out, b_out, ln2_gain, ln2_bias, w_fc, b_fc, w_proj, b_proj):
    tokens, width = inputs.shape[1:]
    count = n_dp * n
    rows = w_qkv.shape[0]
    units = w_proj.shape[0]
    r = n // HEADS
    hd = width // HEADS
    d, me = lax.axis_index("dp"), lax.axis_index("ctx")
    flat = d * n + me
    head = me // r
    both = ("dp", "ctx")
    x, dy = inputs[0], cotangent[0]
    halves = (n_dp // 2, 2, 2, n // 2)

    small = (ln1_gain, ln1_bias, b_qkv, block_ids[0], b_out, ln2_gain, ln2_bias, b_fc, b_proj)
    small = [v.reshape(1, -1) for v in small]

    def heads_of(w):
        w = w.reshape(w.shape[0], 3, HEADS, 1, hd)
        w = jnp.stack([w[:, 0], jnp.zeros_like(w[:, 0]), w[:, 1], w[:, 2]], axis=3)
        return w.reshape(w.shape[0], HEADS, 4 * hd)

    spread = rows % 16 == 0 and units == 128 and r == 1
    if spread:
        got = lead(n_dp, n, x, small, dy, w_qkv, w_fc, w_proj, w_out)
        small_all, first, a, b, o, wq, params = got[:7]
        middle, middle_grad, low, branch, agb, sums4, part_out, wp_grad, wf_grad, bf_grad = got[7:]
        wq = wq.reshape(width, -1)
        grads = (low, branch, wf_grad.reshape(count, rows, -1), wp_grad.reshape(n_dp, units, width))
    else:
        full = lax.all_gather(w_qkv, both, axis=0, tiled=True)
        wq = lax.dynamic_index_in_dim(heads_of(full), head, 1, keepdims=False)
        wf = lax.all_gather(w_fc, both, axis=0, tiled=True).reshape((width,) + halves + (units,))
        wf = lax.dynamic_index_in_dim(wf, d % 2, 2, keepdims=False)
        wf = lax.dynamic_index_in_dim(wf, me % (n // 2), 3, keepdims=False).reshape(width, n_dp * units)
        wp = lax.all_gather(w_proj, both, axis=0, tiled=True).reshape(halves + (units, width))
        wp = lax.dynamic_index_in_dim(wp, d % 2, 1, keepdims=False)
        wp = lax.dynamic_index_in_dim(wp, me % (n // 2), 2, keepdims=False).reshape(n_dp * units, width)
        wo = lax.all_gather(w_out, both, axis=0, tiled=True)
        small_all, first, a, b, o, att, dy_all = front(n_dp, n, r, x, small, dy, wq)

        def vector(row, size):
            return small_all[:, row, :size].astype(F32).reshape(1, -1)

        params = jnp.concatenate([vector(k, rows) for k in (BO, G2, C2, G1, BP)])
        bf = vector(BF, units).reshape(halves + (units,))
        bf = lax.dynamic_index_in_dim(bf, d % 2, 1, keepdims=False)
        bf = lax.dynamic_index_in_dim(bf, me % (n // 2), 2, keepdims=False).reshape(1, -1)
        got = ffn(n, r, att, x, dy, dy_all, wo, wf, wp, bf, params[:3])
        middle, middle_grad, low, branch, agb, sums4, part_out, wp_grad, wf_grad, bf_grad = got
        params, grads = params[3:], None
    got = back(n_dp, n, r, agb, a, b, o, small_all, wq, first, part_out, x, middle, middle_grad, params, sums4, bf_grad, grads)
    if spread:
        return finish(n_dp, n, *got)
    output, input_grad, sums = got[:3]
    owned = lambda v: lax.psum_scatter(v, both, scatter_dimension=0, tiled=True)
    hot = (jnp.arange(2) == d % 2).reshape(1, 2, 1, 1, 1) & (jnp.arange(n // 2) == me % (n // 2)).reshape(1, 1, 1, -1, 1)
    g = got[3].reshape(width, 4, 1, hd)
    g = jnp.stack([g[:, 0], g[:, 2], g[:, 3]], axis=1)
    wq_own = owned(jnp.where((jnp.arange(HEADS) == head).reshape(1, 1, -1, 1), g, 0.0).reshape(width, 3 * width))
    g = wf_grad.astype(F32).reshape(width, n_dp // 2, 1, 2, 1, units)
    wf_own = owned(jnp.where(hot[None], g, 0.0).reshape(width, -1))
    g = wp_grad.astype(F32).reshape(n_dp // 2, 1, 2, 1, units, width)
    wp_own = owned(jnp.where(hot[..., None], g, 0.0).reshape(-1, width))
    wo_own = owned(dot(low, branch, TN))

    cut = lambda k, size: lax.dynamic_slice(sums[k], (flat * size % 128,), (size,))
    g1g, c1g, bog, g2g, c2g, bpg = (cut(k, rows) for k in range(6))
    bqvg = cut(6, 2 * rows)
    group = d // 2 * 2 + me // (n // 2)
    bfg = lax.dynamic_slice(sums[7 : 7 + n_dp * units // 128].reshape(-1), (group * units,), (units,))
    return (
    output[None], input_grad[None], g1g, c1g, wq_own, bqvg, wo_own, bog, g2g, c2g, wf_own, bfg, wp_own, bpg,
    )


def solution(mesh):
    both = ("dp", "ctx")
    act, vec, mat = P("dp", "ctx", None), P(both), P(both, None)
    return jax.shard_map(
    functools.partial(local, mesh.shape["dp"], mesh.shape["ctx"]),
    mesh=mesh,
    in_specs=(act, act, P("dp", "ctx"), vec, vec, mat, vec, mat, vec, vec, vec, mat, vec, mat, vec),
    out_specs=(act, act, vec, vec, mat, vec, mat, vec, vec, vec, mat, vec, mat, vec),
    check_vma=False,
    )
```

profile of v0, /device:TPU:0, one launch (start us, length us, event | category | flops | bytes accessed | tf_op | source)
XLA Modules:
  0.0 242.7 jit_solution(8541616133199858341)
XLA Ops:
  0.7 143.7 %lead.1 = (bf16[32,16,128]{2,1,0:T(8,128)(2,1)}, bf16[2048,1024]{1,0:T(8,128)(2,1)}, bf16[2048,128]{1,0:T(8,128)(2,1)}, bf16[2048,128]{1,0:T(8,128)(2,1)}, f32[2...) custom-call(bf16[128,1024]{1,0:T(8,128)(2,1)} %bitcast.21, ...), custom_call_target="tpu_custom_call" | custom-call | tf_op jit(solution)/shard_map/lead/pallas_call | solution.py:1146
  144.3 95.4 %back.1 = (bf16[128,1024]{1,0:T(8,128)(2,1)}, bf16[128,1024]{1,0:T(8,128)(2,1)}, f32[16,128]{1,0:T(8,128)}, bf16[16,32,256]{2,1,0:T(8,128)(2,1)}, bf16[32,32,256...) custom-call(bf16[16,64,128]{2,1,0:T(8,128)(2,1)} %get-tuple-element.52.refs_0_, ...), custom_call_target="tpu_custom_call" | custom-call | tf_op jit(solution)/shard_map/back/pallas_call | solution.py:1466
  239.8 2.9 %finish.1 = (bf16[1,128,1024]{2,1,0:T(8,128)(2,1)}, bf16[1,128,1024]{2,1,0:T(8,128)(2,1)}, f32[1,32]{1,0:T(1,128)}, f32[1,32]{1,0:T(1,128)}, f32[32,3072]{1,0:T(...) custom-call(bf16[128,1024]{1,0:T(8,128)(2,1)} %get-tuple-element.69., ...), custom_call_target="tpu_custom_call" | custom-call | tf_op jit(solution)/shard_map/finish/pallas_call | solution.py:1519
where the time goes:
time: 243 us
  Pallas kernels  242 us (100%)
    pallas_call x1, Pallas kernels, lead(): pl.pallas_call(functools.partial(lead_kernel, n_dp, n, cube, whole), out_...  144 us
    pallas_call x1, Pallas kernels, back(): pl.pallas_call(functools.partial(back_kernel, n_dp, n, r, spread, cube, w...  95.4 us

commit v1 on v0

--- a/solution.py
+++ b/solution.py
@@ -17,6 +17,7 @@
 MESH = pl.DeviceIdType.MESH
 DMA = pltpu.SemaphoreType.DMA
 VMEM_LIMIT = 60 << 20
+VMEM_MOST = 63 << 20
 
 
 def dot(x, y, dims=(((1,), (0,)), ((), ()))):
@@ -253,12 +254,18 @@
             if k + 1 < self.links:
                 self.link(part, k + 1).start()
 
-    def finish(self):
+    def core_sent(self):
         for half in range(2):
             self.core(half).wait_send()
+
+    def links_sent(self):
         for part in range(len(self.orders)):
             for k in range(self.links):
                 self.link(part, k).wait_send()
+
+    def finish(self):
+        self.core_sent()
+        self.links_sent()
 
 
 class Line:
@@ -853,19 +860,22 @@
     return (normed * prm[G1 : G1 + 1, :] + prm[C1 : C1 + 1, :]).astype(BF16)
 
 
-def lead_kernel(n_dp, n, cube, whole, *refs):
+def layer_kernel(n_dp, n, cube, whole, *refs):
     refs = list(refs)
     take = lambda k: [refs.pop(0) for _ in range(k)]
     x_ref, pieces, (dy_own, w_qkv, w_fc, w_proj, w_out) = refs.pop(0), take(9), take(5)
-    small_all, first_out, a_ref, b_ref, o_ref, wq_all, par_ref = take(7)
-    middle_ref, mg_ref, low_ref, branch_ref, agb, sums_ref, out_hbm, wp_grad, wf_grad, bf_grad = take(10)
+    out_ref, ig_ref, sums, wq_got, wf_got, wp_got, wo_own = take(7)
+    small_all, a_ref, b_ref, o_ref, wq_all, middle_ref, mg_ref, low_ref, branch_ref, agb, wp_grad, wf_grad, bf_grad = take(13)
     xbuf, first, prm, bqv, bias, bf_row, idrow, idcol, packed, acc, tot, att, wqb, wfb = take(14)
-    wf_all, wo_all, wp_ref, dy_ref, sbuf, grads, act, hid, terms, out_ref, sg = take(11)
-    first_sems, out_sems, tile, small_ref = take(4)
+    wf_all, wo_all, wp_ref, dy_ref, sbuf, grads, act, hid, terms, sg, osum, tile, small_ref, sums_ref = take(14)
+    ag, kbuf, ybuf, zbuf, got, msg, wq_part, wq_mine, wq_else = take(9)
     links = len(cube[0]) - 1
-    bufs = take(links + 1)
+    bufs, out_bufs = take(links + 1), take(links + 1)
+    wo_bufs = take(len(whole[0]))
     line_sems, small_sems, dy_sems, att_sems, wq_sems, wf_sems, wo_sems = take(6), take(2), take(4), take(2), take(4), take(2), take(4)
     wp_sems, gather_sems, scatter_sems = take(2), take(4), take(4)
+    ag_sems, back_sems, outs_sems, msg_sems = take(2), take(6), take(4), take(2)
+    wqg_sems, wfg_sems, wpg_sems, wog_sems = take(4), take(2), take(2), take(4)
 
     tokens, width = x_ref.shape
     length = n * tokens
@@ -930,16 +940,11 @@
     for i in range(n_dp):
         owner = (i // 2 * 2 + d % 2) * n + i % 2 * (n // 2) + me % (n // 2)
         bf_row[:, i * units : (i + 1) * units] = small_all[owner].astype(F32)[BF : BF + 1, :units]
-    par_ref[0:1, :] = prm[G1 : G1 + 1, :]
-    par_ref[1:2, :] = prm[BP : BP + 1, :]
     put_ids(n, small_all, d * n, idrow, idcol)
     per_z = n // 4
 
     def plane(slot):
         return pl.ds(pl.multiple_of(line.slots[slot] * per_z * tokens, per_z * tokens), per_z * tokens)
-
-    def save(slot):
-        return pltpu.make_async_copy(first.at[plane(slot)], first_out.at[plane(slot)], first_sems.at[slot])
 
     def project(slot):
         z = line.slots[slot]
@@ -954,7 +959,6 @@
         qkv = (dot(first[at, :], wq_all[...].reshape(width, 256)) + bias[...]).astype(BF16)
         a_ref[at, :] = qkv[:, :128]
         b_ref[at, :] = qkv[:, 128:]
-        save(slot).start()
 
     xg.z_step(1)
     xg.y_step(2)
@@ -1084,14 +1088,12 @@
         wf_grad[at, :] = jnp.transpose(dot(hid[...], low, TN)).astype(BF16)
         wp_grad[:, at] = dot(act[...], dy_ref[..., at].reshape(4 * quarter, 256), TN).astype(BF16)
 
-    def out_copy(i):
-        return pltpu.make_async_copy(out_ref.at[i % 2], out_hbm.at[(i // 2, i % 2) + inner], out_sems.at[i % 2])
-
+    outs = Scatter(cube, terms, out_bufs, outs_sems)
+    s.core_sent()
     for i in range(4):
-        if i >= 2:
-            out_copy(i - 2).wait()
-        out_ref[i % 2] = dot(act[span(i // 2, i % 2), :], wp_ref[...]).astype(BF16).reshape(block)
-        out_copy(i).start()
+        terms[(i // 2, i % 2) + inner] = dot(act[span(i // 2, i % 2), :], wp_ref[...]).astype(BF16).reshape(block)
+    for h in range(2):
+        outs.core(h).start()
     for k in range(links):
         s.step(k, sg)
         if k < 2:
@@ -1110,60 +1112,222 @@
         lo, hi = grad[:half, h * 64 : h * 64 + 128], grad[half:, h * 64 : h * 64 + 128]
         agb[h] = jnp.where(lane < 64, lo, pltpu.roll(hi, 64, 1)).astype(BF16)
         agb[h + 1] = jnp.where(lane < 64, pltpu.roll(lo, 64, 1), hi).astype(BF16)
+    heads = ToAll(n_dp, n, lambda f: agb.at[f], ag, ag_sems, True)
+    heads.start()
+    ag[me] = agb[me]
     column = lambda v: jnp.sum(v, axis=0, keepdims=True)
     sums_ref[0:1, :] = column(branch.astype(F32))
     sums_ref[1:2, :] = column(second_grad * n2)
     sums_ref[2:3, :] = column(second_grad)
     sums_ref[3:4, :] = column(dy)
-    for i in (2, 3):
-        out_copy(i).wait()
-    for slot in range(4):
-        save(slot).wait()
-    for c in (wq, wf, small, out):
+
+    block_of = lambda ref, f, size: ref.at[pl.ds(pl.multiple_of(f * size, size), size)]
+    wfs = ToAll(n_dp, n, lambda f: block_of(wf_grad, f, rows), wf_got, wfg_sems)
+    wqs = ToAll(n_dp, n, lambda f: wq_mine.at[f], wq_got, wqg_sems[:2], True)
+    wo = Scatter(whole, wo_all, wo_bufs, wog_sems)
+    wf_got[flat] = block_of(wf_grad, flat, rows)[...]
+    wp_got[group] = block_of(wp_grad, group, units)[...]
+    wpgs, dpgs = [], []
+    for i in range(1, n_dp):
+        to, peer = group_peer(n, i, n_dp)
+        wpgs.append(remote(block_of(wp_grad, to, units), wp_got.at[group], wpg_sems[0].at[i], wpg_sems[1].at[i], peer))
+        other = (d + i) % n_dp
+        dpgs.append(remote(wq_part.at[other], wq_else.at[i], wqg_sems[2].at[i], wqg_sems[3].at[i], {"dp": other}))
+    for c in wpgs:
+        c.start()
+    for h in range(2):
+        outs.add_core(h)
+    heads.wait_recv()
+    outs.start_links()
+    wfs.start()
+    wog.finish()
+    for k in range(width // 256):
+        part = dot(low_ref[:, k * 256 : (k + 1) * 256], branch, TN).astype(BF16)
+        for i in range(256 // rows):
+            f = k * (256 // rows) + i
+            wo_all[tuple((f >> b) & 1 for b in range(len(whole[0]) - 1, -1, -1))] = part[i * rows : (i + 1) * rows]
+    for h in range(2):
+        wo.core(h).start()
+    mixed, dkv = act, grads
+    dkv[:, :128] = jnp.zeros((length, 128), F32)
+
+    def per_queries_back(gq, _):
+        qs = pl.ds(pl.multiple_of(gq * QB, QB), QB)
+        pieces = []
+        for i in range(QB // tokens):
+            t = ag[gq * (QB // tokens) + i].astype(F32)
+            pieces += [jnp.where(lane >= 64, pltpu.roll(t, 64, 1), 0.0), jnp.where(lane >= 64, t, 0.0)]
+        grad = jnp.concatenate(pieces, axis=0)
+        o = o_ref[qs, :]
+        inverse = 1.0 / o[:, :1]
+        upper = lax.broadcasted_iota(jnp.int32, (QB, 128), 1) >= 64
+        ratio = jnp.sum(jnp.where(upper, grad * o, 0.0), axis=-1, keepdims=True) * inverse
+        ratio = jnp.transpose(jnp.broadcast_to(ratio, (QB, 128)))[:1, :]
+        do = (grad * inverse).astype(BF16)
+        a = a_ref[qs, :]
+        scaled = a * 0.125
+        ado = jnp.concatenate([a, do], axis=0)
+        ids = idrow[:, qs]
+        acc[...] = jnp.zeros_like(acc)
+
+        def per_keys(kb, _):
+            ks = pl.ds(pl.multiple_of(kb * kc, kc), kc)
+            b = b_ref[ks, :]
+            w = jnp.where(idcol[ks, :] <= ids, jnp.exp(dot(b, scaled, NT)), 0.0)
+            t = (w * (dot(b, do, NT) - ratio)).astype(BF16)
+            dkv[ks, :128] += dot(jnp.concatenate([t, w.astype(BF16)], axis=1), ado)
+            acc[...] += dot(t, b, TN)
+            return 0
+
+        lax.fori_loop(0, jnp.minimum(((gq + 2) * QB + kc - 1) // kc, length // kc), per_keys, 0)
+        mixed[qs, :128] = jnp.where(upper, 0.0, acc[...] * 0.125).astype(BF16)
+        return 0
+
+    cuts = [0, blocks // 2, blocks * 3 // 4, blocks]
+    for k in range(3):
+        lax.fori_loop(cuts[k], cuts[k + 1], per_queries_back, 0)
+        if k + 1 < links:
+            outs.step(k, osum)
+    for h in range(2):
+        wo.add_core(h)
+    total = dkv[:, :128]
+    lower = lax.broadcasted_iota(jnp.int32, (length, 128), 1) < 64
+    mixed[:, 128:] = jnp.where(lower, total * 0.125, total).astype(BF16)
+
+    xg.finish()
+    rs = LineScatter(line, xbuf, kbuf, ybuf, zbuf, back_sems)
+
+    def first_grad(slot):
+        part = dot(mixed[plane(slot), :], wq_all[...].reshape(width, 256), NT).astype(BF16)
+        xbuf[line.slots[slot]] = part.reshape(n // 8, 2, tokens, width)
+        rs.core_start(slot)
+
+    first_grad(0)
+    for slot in range(1, 4):
+        first_grad(slot)
+        rs.core_step(slot - 1)
+    rs.core_step(3)
+    for k in range(min(2, links - 1), links):
+        outs.step(k, osum)
+    wo.start_links()
+
+    def wq_grad(i):
+        k = ((d + 1) * (width // 256 // n_dp) + i) % (width // 256)
+        part = jnp.transpose(dot(mixed[...], first[:, pl.ds(pl.multiple_of(k * 256, 256), 256)], TN))
+        q = 256 // rows
+        wq_part[k * q // n, pl.ds(k * q % n, q)] = part.astype(BF16).reshape(q, rows, 256)
+
+    turns = width // 256
+    ahead = turns - turns // n_dp
+    for i in range(ahead):
+        wq_grad(i)
+    for c in dpgs:
+        c.start()
+    rs.z_step(0)
+    for i in range(ahead, turns):
+        wq_grad(i)
+    rs.z_step(1)
+    total = wq_part[d].astype(F32)
+    for i, c in enumerate(dpgs):
+        c.wait_recv()
+        total = total + wq_else[i + 1].astype(F32)
+    wq_mine[...] = total.astype(BF16)
+    wq_got[me] = wq_mine[me]
+    wqs.start()
+    wo.step(0, wo_own)
+    total = jnp.sum(mixed[...].astype(F32), axis=0, keepdims=True)
+    q_row = half_row(total[:, :128], 0, False)
+    q_row = jnp.where(odd == 1, pltpu.roll(q_row, 64, 1), q_row)
+    v_row = half_row(total[:, 128:], 1, True)
+    v_row = jnp.where(odd == 1, v_row, pltpu.roll(v_row, 64, 1))
+    rs.z_step(2)
+    out_ref[...] = (middle_ref[...] + osum[...] + prm[BP : BP + 1, :]).astype(BF16)
+    n1, rstd1 = normalize(x_ref[...].astype(F32))
+    wo.step(1, wo_own)
+
+    def prepare(f, _):
+        at = f * 2 * width // count // 128
+        msg[f, 6:7, :] = jnp.where(at == me // 2, q_row, 0.0) + jnp.where(at == width // 128 + me // 2, v_row, 0.0)
+        same = group_of(n, f)[0] == rank
+        for i in range(bf_grad.shape[1] // 128):
+            msg[f, 7 + i : 8 + i, :] = jnp.where(same, bf_grad[:, i * 128 : (i + 1) * 128], 0.0)
+        return 0
+
+    msg[...] = jnp.zeros_like(msg)
+    lax.fori_loop(0, count, prepare, 0)
+    rs.last(sg)
+
+    grad = sg[...]
+    gain, shift = column(grad * n1), column(grad)
+    per = 128 * count // width
+    for k in range(width // 128):
+        at = slice(k * 128, (k + 1) * 128)
+        lines = jnp.concatenate([gain[:, at], shift[:, at], sums_ref[:, at]], axis=0)
+        for i in range(per):
+            msg[k * per + i, 0:6, :] = lines
+    tell = ToAll(n_dp, n, lambda f: msg.at[f], got, msg_sems)
+    tell.start()
+    got[flat] = msg[flat]
+    ig_ref[...] = (mg_ref[...] + normalize_back(grad * prm[G1 : G1 + 1, :], n1, rstd1)).astype(BF16)
+    for k in range(2, wo.links):
+        wo.step(k, wo_own)
+    wfs.wait_recv()
+    wqs.wait_recv()
+    for c in wpgs:
+        c.wait_recv()
+    tell.wait_recv()
+    sums[...] = jnp.sum(got[...], axis=0)
+    for c in (wq, wf, small, out, heads, wfs, wqs, tell):
         c.wait_send()
-    for c in dps + wps:
+    for c in dps + wps + wpgs + dpgs:
         c.wait_send()
-    for c in (xg, wog, dyg, g, s):
+    s.links_sent()
+    for c in (dyg, g, outs, wo, rs):
         c.finish()
 
 
-def lead(n_dp, n, x, small, dy, w_qkv, w_fc, w_proj, w_out):
+def layer(n_dp, n, x, small, dy, w_qkv, w_fc, w_proj, w_out):
     tokens, width = x.shape
     count, length = n_dp * n, n * tokens
-    rows, units = w_fc.shape[0], n_dp * w_proj.shape[0]
+    rows, own = w_fc.shape[0], w_proj.shape[0]
+    units = n_dp * own
     cube, whole = cube_plan(n, tokens), all_plan(n_dp, n, rows)
     block = (2,) * len(cube[0]) + (tokens, width)
-    shape = jax.ShapeDtypeStruct
-    vm, hbm = pl.BlockSpec(memory_space=pltpu.VMEM), pl.BlockSpec(memory_space=pl.ANY)
+    shape, v = jax.ShapeDtypeStruct, pltpu.VMEM
+    vm = pl.BlockSpec(memory_space=pltpu.VMEM)
     outs = [
-        (shape((count, 16, 128), BF16), vm), (shape((length, width), BF16), hbm), (shape((length, 128), BF16), vm),
-        (shape((length, 128), BF16), vm), (shape((length, 128), F32), vm), (shape((n_dp, n, rows, 256), BF16), vm),
-        (shape((2, width), F32), vm), (shape((tokens, width), F32), vm), (shape((tokens, width), F32), vm),
-        (shape((tokens, width), BF16), vm), (shape((tokens, width), BF16), vm), (shape((n, tokens // 2, 128), BF16), vm),
-        (shape((4, width), F32), vm), (shape(block, BF16), hbm), (shape((units, width), BF16), vm),
-        (shape((width, units), BF16), vm), (shape((1, units), F32), vm),
+        shape((tokens, width), BF16), shape((tokens, width), BF16), shape((16, 128), F32), shape((n, rows, 256), BF16),
+        shape((count, rows, units), BF16), shape((n_dp, own, width), BF16), shape((rows, width), F32),
     ]
+    heads = (n, tokens // 2, 128)
+    all_sems = [DMA((count,))] * 2
+    weight_sems = [DMA((n,))] * 2 + [DMA((n_dp,))] * 2
     return pl.pallas_call(
-        functools.partial(lead_kernel, n_dp, n, cube, whole),
-        out_shape=[o for o, _ in outs],
+        functools.partial(layer_kernel, n_dp, n, cube, whole),
+        out_shape=outs,
         in_specs=[vm] * 15,
-        out_specs=[s for _, s in outs],
+        out_specs=[vm] * len(outs),
         scratch_shapes=[
-            pltpu.VMEM((4, n // 8, 2, tokens, width), BF16), pltpu.VMEM((length, width), BF16), pltpu.VMEM((16, width), F32),
-            pltpu.VMEM((2 * width // 128, 128), F32), pltpu.VMEM((1, 256), F32), pltpu.VMEM((1, units), F32),
-            pltpu.VMEM((1, length), F32), pltpu.VMEM((length, 1), F32), pltpu.VMEM((n, tokens // 2, 128), BF16),
-            pltpu.VMEM((QB, 128), F32), pltpu.VMEM((QB, 128), F32), pltpu.VMEM((n, tokens // 2, 128), BF16),
-            pltpu.VMEM((n, rows, 256), BF16), pltpu.VMEM((n, rows, units), BF16),
-            pltpu.VMEM((count, rows, units), BF16), pltpu.VMEM((2,) * len(whole[0]) + (rows, width), BF16),
-            pltpu.VMEM((units, width), BF16), pltpu.VMEM(block, BF16), pltpu.VMEM(block, BF16),
-            pltpu.VMEM((length, units), F32), pltpu.VMEM((length, units), BF16), pltpu.VMEM((length, units), BF16),
-            pltpu.VMEM(block, BF16), pltpu.VMEM((2,) + block[2:], BF16), pltpu.VMEM((tokens, width), F32), DMA((4,)), DMA((2,)),
-            pltpu.VMEM((16, 128), F32), pltpu.VMEM((16, 128), BF16),
-        ] + Scatter.scratch(cube, tokens, width) + LineGather.sems(n) + [DMA((count,))] * 2 + Gather.sems(cube) + [DMA((n,))] * 2
-        + [DMA((n,))] * 2 + [DMA((n_dp,))] * 2 + [DMA((count,))] * 2 + Gather.sems(whole) + [DMA((n_dp,))] * 2
-        + Gather.sems(cube) + Scatter.sems(cube),
-        compiler_params=pltpu.CompilerParams(collective_id=1, has_side_effects=True, vmem_limit_bytes=VMEM_LIMIT),
-        name="lead",
+            v((count, 16, 128), BF16), v((length, 128), BF16), v((length, 128), BF16), v((length, 128), F32),
+            v((n_dp, n, rows, 256), BF16), v((tokens, width), F32), v((tokens, width), F32), v((tokens, width), BF16),
+            v((tokens, width), BF16), v(heads, BF16), v((units, width), BF16), v((width, units), BF16), v((1, units), F32),
+            v((4, n // 8, 2, tokens, width), BF16), v((length, width), BF16), v((16, width), F32), v((2 * width // 128, 128), F32),
+            v((1, 256), F32), v((1, units), F32), v((1, length), F32), v((length, 1), F32), v(heads, BF16), v((QB, 128), F32),
+            v((QB, 128), F32), v(heads, BF16), v((n, rows, 256), BF16), v((n, rows, units), BF16),
+            v((count, rows, units), BF16), v((2,) * len(whole[0]) + (rows, width), BF16), v((units, width), BF16), v(block, BF16),
+            v(block, BF16), v((length, units), F32), v((length, units), BF16), v((length, units), BF16), v(block, BF16),
+            v((tokens, width), F32), v((tokens, width), F32), v((16, 128), F32), v((16, 128), BF16), v((4, width), F32),
+            v(heads, BF16),
+        ] + LineScatter.scratch(n, tokens, width) + [
+            v((count, 16, 128), F32), v((count, 16, 128), F32), v((n_dp, n, rows, 256), BF16), v((n, rows, 256), BF16),
+            v((n_dp, n, rows, 256), BF16),
+        ] + Scatter.scratch(cube, tokens, width) * 2 + Scatter.scratch(whole, rows, width)
+        + LineGather.sems(n) + all_sems + Gather.sems(cube) + [DMA((n,))] * 2 + weight_sems + all_sems + Gather.sems(whole)
+        + [DMA((n_dp,))] * 2 + Gather.sems(cube) + Scatter.sems(cube)
+        + [DMA((n,))] * 2 + LineScatter.sems(n) + Scatter.sems(cube) + all_sems
+        + weight_sems + all_sems + [DMA((n_dp,))] * 2 + Scatter.sems(whole),
+        compiler_params=pltpu.CompilerParams(collective_id=4, has_side_effects=True, vmem_limit_bytes=VMEM_MOST),
+        name="layer",
     )(x, *small, dy, w_qkv, w_fc, w_proj, w_out)
 
 
@@ -1555,36 +1719,28 @@
 
     spread = rows % 16 == 0 and units == 128 and r == 1
     if spread:
-        got = lead(n_dp, n, x, small, dy, w_qkv, w_fc, w_proj, w_out)
-        small_all, first, a, b, o, wq, params = got[:7]
-        middle, middle_grad, low, branch, agb, sums4, part_out, wp_grad, wf_grad, bf_grad = got[7:]
-        wq = wq.reshape(width, -1)
-        grads = (low, branch, wf_grad.reshape(count, rows, -1), wp_grad.reshape(n_dp, units, width))
-    else:
-        full = lax.all_gather(w_qkv, both, axis=0, tiled=True)
-        wq = lax.dynamic_index_in_dim(heads_of(full), head, 1, keepdims=False)
-        wf = lax.all_gather(w_fc, both, axis=0, tiled=True).reshape((width,) + halves + (units,))
-        wf = lax.dynamic_index_in_dim(wf, d % 2, 2, keepdims=False)
-        wf = lax.dynamic_index_in_dim(wf, me % (n // 2), 3, keepdims=False).reshape(width, n_dp * units)
-        wp = lax.all_gather(w_proj, both, axis=0, tiled=True).reshape(halves + (units, width))
-        wp = lax.dynamic_index_in_dim(wp, d % 2, 1, keepdims=False)
-        wp = lax.dynamic_index_in_dim(wp, me % (n // 2), 2, keepdims=False).reshape(n_dp * units, width)
-        wo = lax.all_gather(w_out, both, axis=0, tiled=True)
-        small_all, first, a, b, o, att, dy_all = front(n_dp, n, r, x, small, dy, wq)
-
-        def vector(row, size):
-            return small_all[:, row, :size].astype(F32).reshape(1, -1)
-
-        params = jnp.concatenate([vector(k, rows) for k in (BO, G2, C2, G1, BP)])
-        bf = vector(BF, units).reshape(halves + (units,))
-        bf = lax.dynamic_index_in_dim(bf, d % 2, 1, keepdims=False)
-        bf = lax.dynamic_index_in_dim(bf, me % (n // 2), 2, keepdims=False).reshape(1, -1)
-        got = ffn(n, r, att, x, dy, dy_all, wo, wf, wp, bf, params[:3])
-        middle, middle_grad, low, branch, agb, sums4, part_out, wp_grad, wf_grad, bf_grad = got
-        params, grads = params[3:], None
-    got = back(n_dp, n, r, agb, a, b, o, small_all, wq, first, part_out, x, middle, middle_grad, params, sums4, bf_grad, grads)
-    if spread:
-        return finish(n_dp, n, *got)
+        return finish(n_dp, n, *layer(n_dp, n, x, small, dy, w_qkv, w_fc, w_proj, w_out))
+    full = lax.all_gather(w_qkv, both, axis=0, tiled=True)
+    wq = lax.dynamic_index_in_dim(heads_of(full), head, 1, keepdims=False)
+    wf = lax.all_gather(w_fc, both, axis=0, tiled=True).reshape((width,) + halves + (units,))
+    wf = lax.dynamic_index_in_dim(wf, d % 2, 2, keepdims=False)
+    wf = lax.dynamic_index_in_dim(wf, me % (n // 2), 3, keepdims=False).reshape(width, n_dp * units)
+    wp = lax.all_gather(w_proj, both, axis=0, tiled=True).reshape(halves + (units, width))
+    wp = lax.dynamic_index_in_dim(wp, d % 2, 1, keepdims=False)
+    wp = lax.dynamic_index_in_dim(wp, me % (n // 2), 2, keepdims=False).reshape(n_dp * units, width)
+    wo = lax.all_gather(w_out, both, axis=0, tiled=True)
+    small_all, first, a, b, o, att, dy_all = front(n_dp, n, r, x, small, dy, wq)
+
+    def vector(row, size):
+        return small_all[:, row, :size].astype(F32).reshape(1, -1)
+
+    params = jnp.concatenate([vector(k, rows) for k in (BO, G2, C2, G1, BP)])
+    bf = vector(BF, units).reshape(halves + (units,))
+    bf = lax.dynamic_index_in_dim(bf, d % 2, 1, keepdims=False)
+    bf = lax.dynamic_index_in_dim(bf, me % (n // 2), 2, keepdims=False).reshape(1, -1)
+    got = ffn(n, r, att, x, dy, dy_all, wo, wf, wp, bf, params[:3])
+    middle, middle_grad, low, branch, agb, sums4, part_out, wp_grad, wf_grad, bf_grad = got
+    got = back(n_dp, n, r, agb, a, b, o, small_all, wq, first, part_out, x, middle, middle_grad, params[3:], sums4, bf_grad, None)
     output, input_grad, sums = got[:3]
     owned = lambda v: lax.psum_scatter(v, both, scatter_dimension=0, tiled=True)
     hot = (jnp.arange(2) == d % 2).reshape(1, 2, 1, 1, 1) & (jnp.arange(n // 2) == me % (n // 2)).reshape(1, 1, 1, -1, 1)

time: 243 us -> 236 us (0.971)
  Pallas kernels: 242 us -> 235 us
    pallas_call x2 -> x1, Pallas kernels: 239 us -> 232 us  [layer(): pl.pallas_call(functools.partial(layer_kernel, n_dp, n, cube, whole), out...]
where the time goes in v1:
time: 236 us
  Pallas kernels  235 us (100%)
    pallas_call x1, Pallas kernels, layer(): pl.pallas_call(functools.partial(layer_kernel, n_dp, n, cube, whole), out...  232 us

profile of v1, /device:TPU:0, one launch (start us, length us, event | category | flops | bytes accessed | tf_op | source)
XLA Modules:
  0.0 236.0 jit_solution(13679421230363604256)
XLA Ops:
  0.7 232.5 %layer.1 = (bf16[128,1024]{1,0:T(8,128)(2,1)}, bf16[128,1024]{1,0:T(8,128)(2,1)}, f32[16,128]{1,0:T(8,128)}, bf16[16,32,256]{2,1,0:T(8,128)(2,1)}, bf16[32,32,25...) custom-call(bf16[128,1024]{1,0:T(8,128)(2,1)} %bitcast.18, bf16[1,32]{1,0:T(2,128)(2,1)} %bitcast.20, ...), custom_call_target="tpu_custom_call" | custom-call | tf_op jit(solution)/shard_map/layer/pallas_call | solution.py:1305
  233.1 2.9 %finish.1 = (bf16[1,128,1024]{2,1,0:T(8,128)(2,1)}, bf16[1,128,1024]{2,1,0:T(8,128)(2,1)}, f32[1,32]{1,0:T(1,128)}, f32[1,32]{1,0:T(1,128)}, f32[32,3072]{1,0:T(...) custom-call(bf16[128,1024]{1,0:T(8,128)(2,1)} %get-tuple-element.35., ...), custom_call_target="tpu_custom_call" | custom-call | tf_op jit(solution)/shard_map/finish/pallas_call | solution.py:1683

commit v2 on v1

--- a/solution.py
+++ b/solution.py
@@ -929,6 +929,8 @@
     wp_ref[pl.ds(pl.multiple_of(group * units, units), units), :] = w_proj[...]
     xg.z_step(0)
     xg.y_step(3)
+    xg.z_step(1)
+    xg.y_step(2)
     wq.wait_recv()
     for c in dps:
         c.start()
@@ -960,15 +962,13 @@
         a_ref[at, :] = qkv[:, :128]
         b_ref[at, :] = qkv[:, 128:]
 
-    xg.z_step(1)
-    xg.y_step(2)
     wog.step(0)
+    xg.z_step(2)
+    xg.y_step(1)
     for c in dps:
         c.wait_recv()
     xg.core_wait(3)
     project(3)
-    xg.z_step(2)
-    xg.y_step(1)
     wog.step(1)
     xg.core_wait(2)
     project(2)
@@ -1100,6 +1100,9 @@
             weight_grads(2 * k)
             weight_grads(2 * k + 1)
 
+    for h in range(2):
+        outs.add_core(h)
+    outs.start_links()
     second_grad = sg[...]
     dy = dy_own[...].astype(F32)
     n2, rstd2 = normalize(middle_ref[...])
@@ -1135,10 +1138,7 @@
         dpgs.append(remote(wq_part.at[other], wq_else.at[i], wqg_sems[2].at[i], wqg_sems[3].at[i], {"dp": other}))
     for c in wpgs:
         c.start()
-    for h in range(2):
-        outs.add_core(h)
     heads.wait_recv()
-    outs.start_links()
     wfs.start()
     wog.finish()
     for k in range(width // 256):

time: 236 us -> 228 us (0.966)
  Pallas kernels: 235 us -> 227 us
    pallas_call x1, Pallas kernels: 232 us -> 224 us  [layer(): pl.pallas_call(functools.partial(layer_kernel, n_dp, n, cube, whole), out...]
where the time goes in v2:
time: 228 us
  Pallas kernels  227 us (100%)
    pallas_call x1, Pallas kernels, layer(): pl.pallas_call(functools.partial(layer_kernel, n_dp, n, cube, whole), out...  224 us

profile of v2, /device:TPU:0, one launch (start us, length us, event | category | flops | bytes accessed | tf_op | source)
XLA Modules:
  0.0 227.8 jit_solution(2536842287603697986)
XLA Ops:
  0.7 224.2 %layer.1 = (bf16[128,1024]{1,0:T(8,128)(2,1)}, bf16[128,1024]{1,0:T(8,128)(2,1)}, f32[16,128]{1,0:T(8,128)}, bf16[16,32,256]{2,1,0:T(8,128)(2,1)}, bf16[32,32,25...) custom-call(bf16[128,1024]{1,0:T(8,128)(2,1)} %bitcast.18, bf16[1,32]{1,0:T(2,128)(2,1)} %bitcast.20, ...), custom_call_target="tpu_custom_call" | custom-call | tf_op jit(solution)/shard_map/layer/pallas_call | solution.py:1305
  224.9 2.9 %finish.1 = (bf16[1,128,1024]{2,1,0:T(8,128)(2,1)}, bf16[1,128,1024]{2,1,0:T(8,128)(2,1)}, f32[1,32]{1,0:T(1,128)}, f32[1,32]{1,0:T(1,128)}, f32[32,3072]{1,0:T(...) custom-call(bf16[128,1024]{1,0:T(8,128)(2,1)} %get-tuple-element.35., ...), custom_call_target="tpu_custom_call" | custom-call | tf_op jit(solution)/shard_map/finish/pallas_call | solution.py:1683

commit v3 on v2

--- a/solution.py
+++ b/solution.py
@@ -976,7 +976,6 @@
     dyg.start()
     for c in wps:
         c.start()
-    wf.start()
     wog.step(2)
     xg.core_wait(1)
     project(1)
@@ -1022,6 +1021,7 @@
     lax.fori_loop(blocks // 2, blocks, per_queries, 0)
     att[me] = packed[me]
     out.start()
+    wf.start()
     for k in range(4, wog.links):
         wog.step(k)
     wog.core_wait()

time: 228 us -> 226 us (level)
  no operation moved by 1% of the time
where the time goes in v3:
time: 226 us
  Pallas kernels  225 us (100%)
    pallas_call x1, Pallas kernels, layer(): pl.pallas_call(functools.partial(layer_kernel, n_dp, n, cube, whole), out...  222 us

profile of v3, /device:TPU:0, one launch (start us, length us, event | category | flops | bytes accessed | tf_op | source)
XLA Modules:
  0.0 225.9 jit_solution(6795560798736999528)
XLA Ops:
  0.7 222.4 %layer.1 = (bf16[128,1024]{1,0:T(8,128)(2,1)}, bf16[128,1024]{1,0:T(8,128)(2,1)}, f32[16,128]{1,0:T(8,128)}, bf16[16,32,256]{2,1,0:T(8,128)(2,1)}, bf16[32,32,25...) custom-call(bf16[128,1024]{1,0:T(8,128)(2,1)} %bitcast.18, bf16[1,32]{1,0:T(2,128)(2,1)} %bitcast.20, ...), custom_call_target="tpu_custom_call" | custom-call | tf_op jit(solution)/shard_map/layer/pallas_call | solution.py:1305
  223.0 2.9 %finish.1 = (bf16[1,128,1024]{2,1,0:T(8,128)(2,1)}, bf16[1,128,1024]{2,1,0:T(8,128)(2,1)}, f32[1,32]{1,0:T(1,128)}, f32[1,32]{1,0:T(1,128)}, f32[32,3072]{1,0:T(...) custom-call(bf16[128,1024]{1,0:T(8,128)(2,1)} %get-tuple-element.35., ...), custom_call_target="tpu_custom_call" | custom-call | tf_op jit(solution)/shard_map/finish/pallas_call | solution.py:1683
